TPU v7x, 256 devices: a whole 4x4x8 slice. The times are simulated.
256 devices in a mesh: grp: 32 (over y, x, core), hd: 8 (over z).
Axes of the slice: x: 4, y: 4, z: 8, core: 2. Of those that a mesh axis runs over, the one named last changes fastest.
Arguments:
- queries: bfloat16 [65536, 1024], P(('grp', 'hd')), may hold values from -8 to 8
- keys: bfloat16 [65536, 1024], P(('grp', 'hd')), may hold values from -8 to 8
- values: bfloat16 [65536, 1024], P(('grp', 'hd')), may hold values from -6 to 6
- grad_out: bfloat16 [65536, 1024], P(('grp', 'hd')), may hold values from -6 to 6
- neighbours: int32 [256, 8], replicated, may hold values from 0 to 255, as said below
Outputs:
- attended: bfloat16 [65536, 1024], P(('grp', 'hd'))
- grad_queries: bfloat16 [65536, 1024], P(('grp', 'hd'))
- grad_keys: bfloat16 [65536, 1024], P(('grp', 'hd'))
- grad_values: bfloat16 [65536, 1024], P(('grp', 'hd'))
Inputs may be any that keep to these rules, and one draw needn't show every extreme that they name: `neighbours`: each block lists 8 distinct blocks, none of its own group (blocks g * 8 to g * 8 + 7 form group g). The blocks of one group list at most one block of any other group, and each block that a group lists is listed by exactly 4 of its blocks.
All inputs are finite; a program needn't handle non-finite values.
Results may differ from a plain program's by a relative error of at most 0.008.
Values may be sent and summed in bfloat16 or wider, within the bound.
A program may use at most 128 MiB of HBM per device.

v0:
```python
import jax
import jax.numpy as jnp
from jax import lax
from jax.sharding import PartitionSpec as P

HEADS = 8


def plan_slots(neighbours, group_index, n_groups, blk_grp):
    listed = neighbours.reshape(n_groups, -1)
    source = listed // blk_grp
    within = listed % blk_grp
    to_group = source == group_index
    own_sources = jnp.take(source, group_index, axis=0)
    picked = jnp.max(jnp.where(to_group, within, 0), axis=1)
    filled = jnp.any(to_group, axis=1)
    return (picked, filled, own_sources)


def score_block(query_blk, key_blk, score_scale):
    return (
        jnp.einsum("qhd,khd->hqk", query_blk, key_blk, preferred_element_type=jnp.float32)
        * score_scale
    )


def finish_block(query_blk, grad_blk, key_parts, value_parts, score_parts, score_scale):
    row_max = score_parts[0].max(axis=2, keepdims=True)
    exp_parts = [jnp.exp(part_scores - row_max) for part_scores in score_parts]
    row_total = jnp.sum(exp_parts[0], axis=2, keepdims=True)
    weight_parts = [part_exp / row_total for part_exp in exp_parts]
    half_parts = [weight.astype(jnp.bfloat16) for weight in weight_parts]
    attended_full = jnp.einsum(
        "hqk,khd->qhd", half_parts[0], value_parts[0], preferred_element_type=jnp.float32
    )
    row_delta = jnp.transpose(jnp.sum(grad_blk.astype(jnp.float32) * attended_full, axis=2))[
        :, :, None
    ]
    grad_query = None
    key_grads = []
    value_grads = []
    for weight, weight_half, key_blk, value_blk in zip(
        weight_parts, half_parts, key_parts, value_parts
    ):
        grad_weights = jnp.einsum(
            "qhd,khd->hqk", grad_blk, value_blk, preferred_element_type=jnp.float32
        )
        grad_scores = (weight * (grad_weights - row_delta)).astype(jnp.bfloat16)
        term = jnp.einsum("hqk,khd->qhd", grad_scores, key_blk, preferred_element_type=jnp.float32)
        grad_query = term
        key_grads.append(
            jnp.einsum("hqk,qhd->khd", grad_scores, query_blk, preferred_element_type=jnp.float32)
            * score_scale
        )
        value_grads.append(
            jnp.einsum("hqk,qhd->khd", weight_half, grad_blk, preferred_element_type=jnp.float32)
        )
    return (
        attended_full,
        grad_query * score_scale,
        jnp.concatenate(key_grads, axis=0),
        jnp.concatenate(value_grads, axis=0),
    )


def on_device(queries, keys, values, grad_out, neighbours):
    full_width = queries.shape[1]
    n_groups = lax.axis_size("grp")
    n_head_dev = lax.axis_size("hd")
    group_index = lax.axis_index("grp")
    heads_here = HEADS // n_head_dev
    head_width = full_width // HEADS
    score_scale = head_width ** (-0.5)
    blk_grp = neighbours.shape[0] // n_groups
    listed_count = neighbours.shape[1]
    query_heads, key_heads, value_heads, grad_heads = (
        lax.all_to_all(queries, "hd", split_axis=1, concat_axis=0, tiled=True),
        lax.all_to_all(keys, "hd", split_axis=1, concat_axis=0, tiled=True),
        lax.all_to_all(values, "hd", split_axis=1, concat_axis=0, tiled=True),
        lax.all_to_all(grad_out, "hd", split_axis=1, concat_axis=0, tiled=True),
    )
    local_width = query_heads.shape[1]
    block_rows = query_heads.shape[0] // blk_grp
    tile_shape = (blk_grp, block_rows, local_width)
    own_keys = key_heads.reshape(tile_shape)
    own_values = value_heads.reshape(tile_shape)
    head_shape = (blk_grp, -1, heads_here, head_width)
    query_tiles = query_heads.reshape(head_shape)
    grad_tiles = grad_heads.reshape(head_shape)
    own_key_tiles = own_keys.reshape(head_shape)
    own_value_tiles = own_values.reshape(head_shape)
    picked, filled, slot_index = plan_slots(neighbours, group_index, n_groups, blk_grp)
    send_keys = jnp.take(own_keys, picked, axis=0)
    send_values = jnp.take(own_values, picked, axis=0)
    got_keys, got_values = (
        lax.all_to_all(send_keys, "grp", split_axis=0, concat_axis=0, tiled=True),
        lax.all_to_all(send_values, "grp", split_axis=0, concat_axis=0, tiled=True),
    )
    near_keys = jnp.take(got_keys, slot_index, axis=0).reshape(head_shape)
    near_values = jnp.take(got_values, slot_index, axis=0).reshape(head_shape)

    def visit_joint(items):
        query_blk, grad_blk, own_k, own_v, near_k, near_v = items
        key_blk = jnp.concatenate([own_k, near_k], axis=0)
        value_blk = jnp.concatenate([own_v, near_v], axis=0)
        return finish_block(
            query_blk,
            grad_blk,
            [key_blk],
            [value_blk],
            [score_block(query_blk, key_blk, score_scale)],
            score_scale,
        )

    outcome = lax.map(
        visit_joint,
        (query_tiles, grad_tiles, own_key_tiles, own_value_tiles, near_keys, near_values),
    )
    attended_full, grad_query, grad_key, grad_value = outcome
    grad_key = grad_key.reshape(blk_grp, 1 + listed_count, block_rows, local_width)
    grad_value = grad_value.reshape(blk_grp, 1 + listed_count, block_rows, local_width)
    empty_slots = jnp.zeros((n_groups, block_rows, local_width), jnp.float32)
    back_keys = empty_slots.at[slot_index].add(grad_key[:, 1:].reshape(-1, block_rows, local_width))
    back_values = empty_slots.at[slot_index].add(
        grad_value[:, 1:].reshape(-1, block_rows, local_width)
    )
    returned_keys, returned_values = (
        lax.all_to_all(
            back_keys.astype(jnp.bfloat16), "grp", split_axis=0, concat_axis=0, tiled=True
        ).astype(back_keys.dtype),
        lax.all_to_all(
            back_values.astype(jnp.bfloat16), "grp", split_axis=0, concat_axis=0, tiled=True
        ).astype(back_values.dtype),
    )
    filled_mask = filled.astype(jnp.float32)[:, None, None]
    total_keys = grad_key[:, 0].at[picked].add(returned_keys * filled_mask)
    total_values = grad_value[:, 0].at[picked].add(returned_values * filled_mask)
    return (
        lax.all_to_all(
            attended_full.astype(jnp.bfloat16).reshape(-1, local_width),
            "hd",
            split_axis=0,
            concat_axis=1,
            tiled=True,
        ),
        lax.all_to_all(
            grad_query.astype(jnp.bfloat16).reshape(-1, local_width),
            "hd",
            split_axis=0,
            concat_axis=1,
            tiled=True,
        ),
        lax.all_to_all(
            total_keys.astype(jnp.bfloat16).reshape(-1, local_width),
            "hd",
            split_axis=0,
            concat_axis=1,
            tiled=True,
        ),
        lax.all_to_all(
            total_values.astype(jnp.bfloat16).reshape(-1, local_width),
            "hd",
            split_axis=0,
            concat_axis=1,
            tiled=True,
        ),
    )


def solution(mesh):
    in_specs = (
        P(("grp", "hd"), None),
        P(("grp", "hd"), None),
        P(("grp", "hd"), None),
        P(("grp", "hd"), None),
        P(),
    )
    out_specs = (
        P(("grp", "hd"), None),
        P(("grp", "hd"), None),
        P(("grp", "hd"), None),
        P(("grp", "hd"), None),
    )
    return jax.shard_map(
        on_device, mesh=mesh, in_specs=in_specs, out_specs=out_specs, check_vma=False
    )
```

profile of v0, /device:TPU:1, one launch (start us, length us, event | category | flops | bytes accessed | tf_op | source)
XLA Modules:
  0.0 506.1 jit_solution(2766379691929118938)
XLA Ops:
  0.7 2.1 copy.37
  2.8 9.0 %all-to-all-start = ((bf16[256,8,128]{0,2,1:T(8,128)(2,1)}), bf16[256,8,128]{0,2,1:T(8,128)(2,1)S(1)}, u32[]{:S(2)}, u32[]{:S(2)}) async-start(bf16[256,8,128]{0,2,1:T(8,128)(2,1)} %bitcast.22), calls=%async_computation | async-start | bytes 1048576 | tf_op jit(solution)/shard_map/all_to_all | solution.py:79
  12.8 17.0 %all-to-all-done = bf16[256,8,128]{0,2,1:T(8,128)(2,1)S(1)} async-done(((bf16[256,8,128]{0,2,1:T(8,128)(2,1)}), bf16[256,8,128]{0,2,1:T(8,128)(2,1)S(1)}, u32[]{:S(2)}, u32[]{:S(2)}) %all-to-all-start) | async-done | bytes 524320 | tf_op jit(solution)/shard_map/all_to_all | solution.py:79
  29.7 4.1 all-to-all-start.3
  35.2 16.7 %all-to-all-done.3 = bf16[256,8,128]{0,2,1:T(8,128)(2,1)} async-done(((bf16[256,8,128]{0,2,1:T(8,128)(2,1)}), bf16[256,8,128]{0,2,1:T(8,128)(2,1)}, u32[]{:S(2)}, u32[]{:S(2)}) %all-to-all-start.3) | async-done | bytes 524320 | tf_op jit(solution)/shard_map/all_to_all | solution.py:78
  51.9 4.2 all-to-all-start.2
  56.7 3.0 gather_fusion.2
  59.8 4.0 broadcast_select_fusion.2
  63.8 10.2 %all-to-all-done.2 = bf16[256,8,128]{0,2,1:T(8,128)(2,1)} async-done(((bf16[256,8,128]{0,2,1:T(8,128)(2,1)}), bf16[256,8,128]{0,2,1:T(8,128)(2,1)}, u32[]{:S(2)}, u32[]{:S(2)}) %all-to-all-start.2) | async-done | bytes 524320 | tf_op jit(solution)/shard_map/all_to_all | solution.py:77
  74.0 35.9 %all_to_all.154 = bf16[32,256,128]{1,2,0:T(8,128)(2,1)S(1)} all-to-all(bf16[32,256,128]{1,2,0:T(8,128)(2,1)} %get-tuple-element.146), channel_id=1, replica_groups=mesh['grp'=32,'hd'=8] {'grp'}, dimensions={0} | all-to-all | bytes 4194304 | tf_op jit(solution)/shard_map/all_to_all | solution.py:97
  109.8 4.9 all-to-all-start.4
  116.0 27.1 %all-to-all-done.4 = bf16[32,256,128]{1,2,0:T(8,128)(2,1)} async-done(((bf16[32,256,128]{1,2,0:T(8,128)(2,1)}), bf16[32,256,128]{1,2,0:T(8,128)(2,1)}, u32[]{:S(2)}, u32[]{:S(2)}) %all-to-all-start.4) | async-done | bytes 2097184 | tf_op jit(solution)/shard_map/all_to_all | solution.py:96
  143.1 4.2 all-to-all-start.5
  147.3 2.9 gather_fusion.1
  150.2 4.4 gather_fusion.3
  154.6 5.9 %broadcast_select_fusion = (bf16[64,256,128]{1,2,0:T(8,128)(2,1)}, bf16[64,256,128]{1,2,0:T(8,128)(2,1)}) fusion(bf16[64,256,128]{1,2,0:T(8,128)(2,1)} %gather_fusion.3, pred[64]{0:T(512)(128)(4,1)S(1)} %compare_and_fusion, bf16[64,256,128]{1,2,0:T(8,128)(2,1)} %gather_fusion.1), kind=kLoop, calls=%fused_computation.53 | loop fusion | flops 4194304 | bytes 16777280 | tf_op jit(solution)/shard_map/jit(_take)/select_n | solution.py:99
  160.5 6.4 %copy.40 = bf16[64,256,128]{2,1,0:T(8,128)(2,1)} copy(bf16[64,256,128]{1,2,0:T(8,128)(2,1)} %get-tuple-element.144) | data formatting | bytes 8388608 | tf_op jit(solution)/shard_map/jit(_take)/select_n | solution.py:100
  166.9 6.4 %copy.45 = bf16[64,256,128]{2,1,0:T(8,128)(2,1)} copy(bf16[64,256,128]{1,2,0:T(8,128)(2,1)} %get-tuple-element.143) | data formatting | bytes 8388608 | tf_op jit(solution)/shard_map/jit(_take)/select_n | solution.py:99
  173.3 148.3 %while.17 = (s32[]{:T(128)}, bf16[8,256,1,128]{1,3,2,0:T(8,128)(2,1)}, bf16[8,256,1,128]{1,3,2,0:T(8,128)(2,1)}, f32[8,2304,1,128]{3,1,0,2:T(8,128)}, f32[8,2304...) while((s32[]{:T(128)}, ...), condition=%wide.region_6.9_spmd, body=%wide.region_2.8_spmd.sunk | while | flops 917601536 | bytes 56044896 | solution.py:115
  173.3 1.5 dynamic-slice_bitcast_fusion.3
  182.9 2.2 fusion.65
  185.2 1.6 copy.85
  191.9 1.5 dynamic-slice_bitcast_fusion.3
  201.5 2.2 fusion.65
  203.7 1.6 copy.85
  210.4 1.5 dynamic-slice_bitcast_fusion.3
  220.0 2.2 fusion.65
  222.2 1.6 copy.85
  228.9 1.5 dynamic-slice_bitcast_fusion.3
  238.5 2.2 fusion.65
  240.7 1.6 copy.85
  247.4 1.5 dynamic-slice_bitcast_fusion.3
  257.0 2.2 fusion.65
  259.2 1.6 copy.85
  266.0 1.5 dynamic-slice_bitcast_fusion.3
  275.6 2.2 fusion.65
  277.8 1.6 copy.85
  284.5 1.5 dynamic-slice_bitcast_fusion.3
  294.1 2.2 fusion.65
  296.4 1.6 copy.85
  303.1 1.5 dynamic-slice_bitcast_fusion.3
  312.7 2.2 fusion.65
  314.9 1.6 copy.85
  321.7 6.5 %all-to-all-start.6 = ((bf16[8,256,128]{1,2,0:T(8,128)(2,1)}), bf16[8,256,128]{1,2,0:T(8,128)(2,1)S(1)}, u32[]{:S(2)}, u32[]{:S(2)}) async-start(bf16[8,256,128]{1,2,0:T(8,128)(2,1)} %bitcast.183), calls=%async_computation.6 | async-start | bytes 1048576 | tf_op jit(solution)/shard_map/all_to_all | solution.py:139
  328.2 7.7 %slice.34 = f32[8,8,256,128]{3,2,1,0:T(8,128)} slice(f32[8,9,256,128]{3,2,1,0:T(8,128)} %bitcast.174), slice={[0:8], [1:9], [0:256], [0:128]} | slice | bytes 16777216 | tf_op jit(solution)/shard_map/slice | solution.py:125
  335.9 2.5 broadcast_in_dim.59.clone
  338.5 19.1 %scatter_fusion.2 = f32[32,256,128]{2,1,0:T(8,128)} fusion(f32[32,256,128]{2,1,0:T(8,128)} %broadcast_in_dim.59.clone, s32[64]{0:T(128)S(1)} %get-tuple-element.131, f32[64,256,128]{2,1,0:T(8,128)} %bitcast.165), kind=kCustom, calls=%fused_computation.6 | custom fusion | flops 2097152 | bytes 25166080 | tf_op jit(solution)/shard_map/scatter-add | solution.py:124
  357.6 3.8 convert_element_type.59
  361.4 6.7 %all-to-all-start.10 = ((bf16[32,256,128]{2,1,0:T(8,128)(2,1)}), bf16[32,256,128]{2,1,0:T(8,128)(2,1)S(1)}, u32[]{:S(2)}, u32[]{:S(2)}) async-start(bf16[32,256,128]{2,1,0:T(8,128)(2,1)} %convert_element_type.59), calls=%async_computation.10 | async-start | bytes 4194304 | tf_op jit(solution)/shard_map/all_to_all | solution.py:131
  368.1 7.7 %slice.32 = f32[8,8,256,128]{3,2,1,0:T(8,128)} slice(f32[8,9,256,128]{3,2,1,0:T(8,128)} %bitcast.172), slice={[0:8], [1:9], [0:256], [0:128]} | slice | bytes 16777216 | tf_op jit(solution)/shard_map/slice | solution.py:123
  375.9 2.5 broadcast_in_dim.59.clone.1
  378.4 19.1 %scatter_fusion = f32[32,256,128]{2,1,0:T(8,128)} fusion(f32[32,256,128]{2,1,0:T(8,128)} %broadcast_in_dim.59.clone.1, s32[64]{0:T(128)S(1)} %get-tuple-element.131, f32[64,256,128]{2,1,0:T(8,128)} %bitcast.164), kind=kCustom, calls=%fused_computation.4 | custom fusion | flops 2097152 | bytes 25166080 | tf_op jit(solution)/shard_map/scatter-add | solution.py:123
  397.5 3.8 convert_element_type.55
  401.4 35.8 %all_to_all.155 = bf16[32,256,128]{2,1,0:T(8,128)(2,1)} all-to-all(bf16[32,256,128]{2,1,0:T(8,128)(2,1)} %convert_element_type.55), channel_id=1, replica_groups=mesh['grp'=32,'hd'=8] {'grp'}, dimensions={0} | all-to-all | bytes 4194304 | tf_op jit(solution)/shard_map/all_to_all | solution.py:128
  437.2 6.9 %all-to-all-start.7 = ((bf16[8,256,128]{1,2,0:T(8,128)(2,1)}), bf16[8,256,128]{1,2,0:T(8,128)(2,1)}, u32[]{:S(2)}, u32[]{:S(2)}) async-start(bf16[8,256,128]{1,2,0:T(8,128)(2,1)} %bitcast.116), calls=%async_computation.7 | async-start | bytes 1048576 | tf_op jit(solution)/shard_map/all_to_all | solution.py:146
  446.2 4.5 convert_multiply_fusion.1
  450.8 6.4 %scatter_fusion.3 = f32[8,256,128]{2,1,0:T(8,128)S(1)} fusion(f32[8,256,128]{2,1,0:T(8,128)S(1)} %slice_bitcast_fusion, s32[32]{0:T(128)S(1)} %fusion.33, f32[32,256,128]{2,1,0:T(8,128)} %get-tuple-element.141), kind=kCustom, calls=%fused_computation.7 | custom fusion | flops 1048576 | bytes 12583040 | tf_op jit(solution)/shard_map/scatter-add | solution.py:137
  458.1 4.0 all-to-all-done.7
  462.2 3.5 all-to-all-start.11
  467.0 6.4 %scatter_fusion.1 = f32[8,256,128]{2,1,0:T(8,128)S(1)} fusion(f32[8,256,128]{2,1,0:T(8,128)S(1)} %slice_bitcast_fusion.1, s32[32]{0:T(128)S(1)} %fusion.33, f32[32,256,128]{2,1,0:T(8,128)} %get-tuple-element.142), kind=kCustom, calls=%fused_computation.5 | custom fusion | flops 1048576 | bytes 12583040 | tf_op jit(solution)/shard_map/scatter-add | solution.py:136
  474.3 9.2 %all-to-all-done.11 = bf16[8,256,128]{2,1,0:T(8,128)(2,1)S(1)} async-done(((bf16[8,256,128]{2,1,0:T(8,128)(2,1)}), bf16[8,256,128]{2,1,0:T(8,128)(2,1)S(1)}, u32[]{:S(2)}, u32[]{:S(2)}) %all-to-all-start.11) | async-done | bytes 524320 | tf_op jit(solution)/shard_map/all_to_all | solution.py:160
  483.5 3.5 all-to-all-start.9
  488.1 2.0 copy.69
  491.3 13.6 %all-to-all-done.9 = bf16[8,256,128]{2,1,0:T(8,128)(2,1)S(1)} async-done(((bf16[8,256,128]{2,1,0:T(8,128)(2,1)}), bf16[8,256,128]{2,1,0:T(8,128)(2,1)S(1)}, u32[]{:S(2)}, u32[]{:S(2)}) %all-to-all-start.9) | async-done | bytes 524320 | tf_op jit(solution)/shard_map/all_to_all | solution.py:153
  (293 shorter events, 117.5 us)
Async XLA Ops:
  0.6 11.2 %copy-start.11 = (bf16[256,1024]{1,0:T(8,128)(2,1)S(1)}, bf16[256,1024]{1,0:T(8,128)(2,1)}, u32[]{:S(2)}) copy-start(bf16[256,1024]{1,0:T(8,128)(2,1)} %param.12) | copy-start | bytes 1572868
  0.6 33.3 %copy-start.14 = (s32[256,8]{0,1:T(8,128)S(1)}, s32[256,8]{0,1:T(8,128)}, u32[]{:S(2)}) copy-start(s32[256,8]{0,1:T(8,128)} %param.15) | copy-start | bytes 24580
  0.7 33.4 %copy-start.12 = (bf16[256,1024]{1,0:T(8,128)(2,1)S(1)}, bf16[256,1024]{1,0:T(8,128)(2,1)}, u32[]{:S(2)}) copy-start(bf16[256,1024]{1,0:T(8,128)(2,1)} %param.11) | copy-start | bytes 1572868
  2.8 27.0 %all-to-all-start = ((bf16[256,8,128]{0,2,1:T(8,128)(2,1)}), bf16[256,8,128]{0,2,1:T(8,128)(2,1)S(1)}, u32[]{:S(2)}, u32[]{:S(2)}) async-start(bf16[256,8,128]{0,2,1:T(8,128)(2,1)} %bitcast.22), calls=%async_computation | async-start | bytes 1048576 | tf_op jit(solution)/shard_map/all_to_all | solution.py:79
  29.7 22.1 %all-to-all-start.3 = ((bf16[256,8,128]{0,2,1:T(8,128)(2,1)}), bf16[256,8,128]{0,2,1:T(8,128)(2,1)}, u32[]{:S(2)}, u32[]{:S(2)}) async-start(bf16[256,8,128]{0,2,1:T(8,128)(2,1)} %bitcast.31), calls=%async_computation.3 | async-start | bytes 1048576 | tf_op jit(solution)/shard_map/all_to_all | solution.py:78
  51.9 22.1 %all-to-all-start.2 = ((bf16[256,8,128]{0,2,1:T(8,128)(2,1)}), bf16[256,8,128]{0,2,1:T(8,128)(2,1)}, u32[]{:S(2)}, u32[]{:S(2)}) async-start(bf16[256,8,128]{0,2,1:T(8,128)(2,1)} %bitcast.28), calls=%async_computation.2 | async-start | bytes 1048576 | tf_op jit(solution)/shard_map/all_to_all | solution.py:77
  109.8 5.1 %copy-start.13 = (bf16[256,1024]{1,0:T(8,128)(2,1)S(1)}, bf16[256,1024]{1,0:T(8,128)(2,1)}, u32[]{:S(2)}) copy-start(bf16[256,1024]{1,0:T(8,128)(2,1)} %param.14) | copy-start | bytes 1572868
  109.8 33.2 %all-to-all-start.4 = ((bf16[32,256,128]{1,2,0:T(8,128)(2,1)}), bf16[32,256,128]{1,2,0:T(8,128)(2,1)}, u32[]{:S(2)}, u32[]{:S(2)}) async-start(bf16[32,256,128]{1,2,0:T(8,128)(2,1)} %get-tuple-element.145), calls=%async_computation.4 | async-start | bytes 4194304 | tf_op jit(solution)/shard_map/all_to_all | solution.py:96
  143.1 30.3 %all-to-all-start.5 = ((bf16[256,8,128]{0,2,1:T(8,128)(2,1)}), bf16[256,8,128]{0,2,1:T(8,128)(2,1)}, u32[]{:S(2)}, u32[]{:S(2)}) async-start(bf16[256,8,128]{0,2,1:T(8,128)(2,1)} %bitcast.36), calls=%async_computation.5 | async-start | bytes 1048576 | tf_op jit(solution)/shard_map/all_to_all | solution.py:80
  173.3 4.0 copy-start.4
  174.8 2.5 copy-start.2
  175.9 1.5 copy-start.7
  189.1 1.5 copy-start.1
  189.5 1.2 copy-start.3
  189.5 2.4 copy-start.5
  191.9 4.0 copy-start.4
  193.3 2.5 copy-start.2
  194.4 1.5 copy-start.7
  207.6 1.5 copy-start.1
  208.0 1.2 copy-start.3
  208.0 2.4 copy-start.5
  210.4 4.0 copy-start.4
  211.8 2.5 copy-start.2
  212.9 1.5 copy-start.7
  226.1 1.6 copy-start.1
  226.5 1.2 copy-start.3
  226.5 2.4 copy-start.5
  228.9 4.0 copy-start.4
  230.4 2.5 copy-start.2
  231.4 1.5 copy-start.7
  244.6 1.5 copy-start.1
  245.0 1.2 copy-start.3
  245.0 2.4 copy-start.5
  247.4 4.0 copy-start.4
  248.9 2.5 copy-start.2
  249.9 1.5 copy-start.7
  263.2 1.5 copy-start.1
  263.6 1.2 copy-start.3
  263.6 2.4 copy-start.5
  266.0 4.0 copy-start.4
  267.4 2.5 copy-start.2
  268.5 1.5 copy-start.7
  281.8 1.6 copy-start.1
  282.1 1.2 copy-start.3
  282.2 2.4 copy-start.5
  284.5 4.0 copy-start.4
  286.0 2.5 copy-start.2
  287.1 1.5 copy-start.7
  300.3 1.5 copy-start.1
  300.7 1.2 copy-start.3
  300.7 2.4 copy-start.5
  303.1 4.0 copy-start.4
  304.5 2.5 copy-start.2
  305.6 1.5 copy-start.7
  318.9 1.6 copy-start.1
  319.3 2.4 copy-start.5
  321.7 39.7 %all-to-all-start.6 = ((bf16[8,256,128]{1,2,0:T(8,128)(2,1)}), bf16[8,256,128]{1,2,0:T(8,128)(2,1)S(1)}, u32[]{:S(2)}, u32[]{:S(2)}) async-start(bf16[8,256,128]{1,2,0:T(8,128)(2,1)} %bitcast.183), calls=%async_computation.6 | async-start | bytes 1048576 | tf_op jit(solution)/shard_map/all_to_all | solution.py:139
  361.4 14.5 %copy-start.9 = (bf16[8,256,128]{1,2,0:T(8,128)(2,1)}, bf16[8,256,128]{1,2,0:T(8,128)(2,1)S(1)}, u32[]{:S(2)}) copy-start(bf16[8,256,128]{1,2,0:T(8,128)(2,1)S(1)} %all-to-all-done.6) | copy-start | bytes 1572868
  361.4 40.0 %all-to-all-start.10 = ((bf16[32,256,128]{2,1,0:T(8,128)(2,1)}), bf16[32,256,128]{2,1,0:T(8,128)(2,1)S(1)}, u32[]{:S(2)}, u32[]{:S(2)}) async-start(bf16[32,256,128]{2,1,0:T(8,128)(2,1)} %convert_element_type.59), calls=%async_computation.10 | async-start | bytes 4194304 | tf_op jit(solution)/shard_map/all_to_all | solution.py:131
  437.2 25.0 %all-to-all-start.7 = ((bf16[8,256,128]{1,2,0:T(8,128)(2,1)}), bf16[8,256,128]{1,2,0:T(8,128)(2,1)}, u32[]{:S(2)}, u32[]{:S(2)}) async-start(bf16[8,256,128]{1,2,0:T(8,128)(2,1)} %bitcast.116), calls=%async_computation.7 | async-start | bytes 1048576 | tf_op jit(solution)/shard_map/all_to_all | solution.py:146
  444.3 1.9 copy-start.6
  462.2 21.4 %all-to-all-start.11 = ((bf16[8,256,128]{2,1,0:T(8,128)(2,1)}), bf16[8,256,128]{2,1,0:T(8,128)(2,1)S(1)}, u32[]{:S(2)}, u32[]{:S(2)}) async-start(bf16[8,256,128]{2,1,0:T(8,128)(2,1)} %convert_element_type.61), calls=%async_computation.11 | async-start | bytes 1048576 | tf_op jit(solution)/shard_map/all_to_all | solution.py:160
  473.4 13.6 %copy-start.10 = (bf16[8,256,128]{1,2,0:T(8,128)(2,1)S(1)}, bf16[8,256,128]{1,2,0:T(8,128)(2,1)}, u32[]{:S(2)}) copy-start(bf16[8,256,128]{1,2,0:T(8,128)(2,1)} %copy-done.9) | copy-start | bytes 1572868
  483.5 21.4 %all-to-all-start.9 = ((bf16[8,256,128]{2,1,0:T(8,128)(2,1)}), bf16[8,256,128]{2,1,0:T(8,128)(2,1)S(1)}, u32[]{:S(2)}, u32[]{:S(2)}) async-start(bf16[8,256,128]{2,1,0:T(8,128)(2,1)} %convert_element_type.58), calls=%async_computation.9 | async-start | bytes 1048576 | tf_op jit(solution)/shard_map/all_to_all | solution.py:153
  (17 other events, 19.1 us)
where the time goes:
time: 511 us; the launch traced here: 506 us
  local copies, waits for them, and re-layouts  122 us (24%)
  waiting for transfers between devices  97.8 us (19%)
  other arithmetic  90.5 us (18%)
  blocking collectives  71.7 us (14%)
  matrix products  68.5 us (13%)
  starting transfers between devices  53.5 us (10%)
    scatter-add x2, other arithmetic, on_device(): empty_slots.at[slot_index]  38.3 us
    all_to_all x1, blocking collectives, on_device(): lax.all_to_all(send_values, 'grp', split_axis=0, concat_axis=0, tiled=True)  35.9 us
    all_to_all x1, blocking collectives, on_device(): lax.all_to_all(back_keys.astype(jnp.bfloat16), 'grp', split_axis=0, conca...  35.8 us
    dynamic_update_slice x32, local copies, waits for them, and re-layouts, on_device(): lax.map(visit_joint, (query_tiles, grad_tiles, own_key_tiles, own_value_t...  33.8 us
    all_to_all x1, waiting for transfers between devices, on_device(): lax.all_to_all(send_keys, 'grp', split_axis=0, concat_axis=0, tiled=True)  27.1 us
    dot_general x8, matrix products, finish_block(): jnp.einsum('hqk,qhd->khd', grad_scores, query_blk, preferred_element_type...  17.9 us
    all_to_all x1, waiting for transfers between devices, on_device(): lax.all_to_all(values, 'hd', split_axis=1, concat_axis=0, tiled=True)  17 us
    all_to_all x1, waiting for transfers between devices, on_device(): lax.all_to_all(keys, 'hd', split_axis=1, concat_axis=0, tiled=True)  16.7 us
  transfers between devices with their start and end apart: 10, of which 7 were waited for; matrix products, arithmetic and copies ran while one was open for 26% of the time, Pallas kernels for 0%

commit v1 on v0

v1 whole, which is shorter than its diff:
```python
import jax
import jax.numpy as jnp
from jax import lax
from jax.experimental import pallas as pl
from jax.experimental.pallas import tpu as pltpu
from jax.sharding import PartitionSpec as P

MESH = pl.DeviceIdType.MESH
HD = 8
GRP = 32
ROWS = 256
W = 128
F32 = jnp.float32
BF16 = jnp.bfloat16
SCALE = W ** (-0.5)

PLACES = [(0, 1), (1, 0), (0, 3), (3, 0), (0, 2), (2, 0), (1, 1), (3, 3), (1, 3), (3, 1), (2, 2), (1, 2), (2, 1), (3, 2), (2, 3), (0, 0)]
XY_ORDER = [dy * 8 + dx * 2 + dc for dc in (0, 1) for dy, dx in PLACES if dy + dx + dc > 0]
Z_ORDER = [1, 7, 2, 6, 3, 5, 4]


def opposite(r):
    return ((4 - r // 8) % 4) * 8 + ((4 - (r // 2) % 4) % 4) * 2 + r % 2


def xy_group(g, r):
    c, x, y = g % 2, (g // 2) % 4, g // 8
    return (((y + r // 8) % 4) * 4 + (x + (r // 2) % 4) % 4) * 2 + (c + r % 2) % 2


def greet(g, z):
    barrier = pltpu.get_barrier_semaphore()
    for r in XY_ORDER:
        pl.semaphore_signal(barrier, inc=1, device_id={"grp": xy_group(g, r), "hd": z}, device_id_type=MESH)
    for d in Z_ORDER:
        pl.semaphore_signal(barrier, inc=1, device_id={"grp": g, "hd": (z + d) % HD}, device_id_type=MESH)
    pl.semaphore_wait(barrier, len(XY_ORDER) + len(Z_ORDER))


HALF = ROWS // 2
IN_PARTS = [("k", 0, HALF), ("k", HALF, HALF), ("v", 0, ROWS)]
OUT_PARTS = [("k", 0, ROWS), ("v", 0, HALF), ("v", HALF, HALF)]


def gather_kernel(picked, q, k, v, do, qh, kh, vh, doh, kgot, vgot, *scr):
    np_ = len(IN_PARTS)
    bufs, sends = scr[:np_], scr[np_ : 2 * np_]
    zs, zr, xs, xr, ls = scr[2 * np_ :]
    g, z = lax.axis_index("grp"), lax.axis_index("hd")
    greet(g, z)
    src = {"k": k, "v": v}
    own_out = {"k": kh, "v": vh}
    got = {"k": kgot, "v": vgot}
    mine = pl.ds(pl.multiple_of(z * W, W), W)

    jobs = [(src[a], r0, n, bufs[i].at[z]) for i, (a, r0, n) in enumerate(IN_PARTS)]
    jobs += [(q, 0, ROWS, qh.at[z]), (do, 0, ROWS, doh.at[z])]

    def z_copy(j, i, d):
        s, r0, n, dst = jobs[j]
        t = (z + d) % HD
        return pltpu.make_async_remote_copy(
            src_ref=s.at[pl.ds(r0, n), pl.ds(pl.multiple_of(t * W, W), W)],
            dst_ref=dst,
            send_sem=zs.at[j, i],
            recv_sem=zr.at[j, i],
            device_id={"grp": g, "hd": t},
            device_id_type=MESH,
        )

    def own_copy(j):
        s, r0, n, dst = jobs[j]
        return pltpu.make_async_copy(s.at[pl.ds(r0, n), mine], dst, ls.at[j])

    for j in range(len(jobs)):
        own_copy(j).start()
        for i, d in enumerate(Z_ORDER):
            z_copy(j, i, d).start()

    def xy_copy(p, i):
        a, r0, n = IN_PARTS[p]
        r = XY_ORDER[i]
        return pltpu.make_async_remote_copy(
            src_ref=sends[p].at[r],
            dst_ref=got[a].at[opposite(r), pl.ds(r0, n)],
            send_sem=xs.at[p, i],
            recv_sem=xr.at[p, i],
            device_id={"grp": xy_group(g, r), "hd": z},
            device_id_type=MESH,
        )

    def keep_copy(p):
        a, r0, n = IN_PARTS[p]
        return pltpu.make_async_copy(bufs[p], own_out[a].at[:, pl.ds(r0, n)], ls.at[len(jobs) + p])

    for p in range(np_):
        own_copy(p).wait()
        for i, d in enumerate(Z_ORDER):
            z_copy(p, i, d).wait_recv()
        for i, r in enumerate(XY_ORDER):
            sends[p][r] = bufs[p][picked[xy_group(g, r)]]
        for i in range(len(XY_ORDER)):
            xy_copy(p, i).start()
        keep_copy(p).start()
    for j in range(np_, len(jobs)):
        own_copy(j).wait()
        for i, d in enumerate(Z_ORDER):
            z_copy(j, i, d).wait_recv()
    for j in range(len(jobs)):
        for i, d in enumerate(Z_ORDER):
            z_copy(j, i, d).wait_send()
    for p in range(np_):
        keep_copy(p).wait()
        for i in range(len(XY_ORDER)):
            xy_copy(p, i).wait_send()
            xy_copy(p, i).wait_recv()


def gather(picked, q, k, v, do):
    hbm = pl.BlockSpec(memory_space=pl.ANY)
    tile = jax.ShapeDtypeStruct((HD, ROWS, W), BF16)
    slots = jax.ShapeDtypeStruct((GRP, ROWS, W), BF16)
    nj, np_ = len(IN_PARTS) + 2, len(IN_PARTS)
    dma = pltpu.SemaphoreType.DMA
    return pl.pallas_call(
        gather_kernel,
        name="gather",
        out_shape=(tile, tile, tile, tile, slots, slots),
        in_specs=[pl.BlockSpec(memory_space=pltpu.SMEM)] + [hbm] * 4,
        out_specs=(hbm,) * 6,
        scratch_shapes=[pltpu.VMEM((HD, n, W), BF16) for _, _, n in IN_PARTS]
        + [pltpu.VMEM((GRP, n, W), BF16) for _, _, n in IN_PARTS]
        + [dma((nj, 7)), dma((nj, 7)), dma((np_, 31)), dma((np_, 31)), dma((nj + np_,))],
        compiler_params=pltpu.CompilerParams(collective_id=0, has_side_effects=True),
    )(picked, q, k, v, do)


def dot(a, b, ca, cb):
    return lax.dot_general(a, b, (((ca,), (cb,)), ((), ())), preferred_element_type=F32)


def attend_kernel(slot, picked, q, do, ko, vo, kg, vg, att, dq, dko, dvo, bk, bv, order, keep, last, has, acc_k, acc_v, e, ph):
    b = pl.program_id(0)
    nb = 9

    @pl.when(b == 0)
    def _():
        acc_k[...] = jnp.zeros_like(acc_k)
        acc_v[...] = jnp.zeros_like(acc_v)

        def by_block(blk, n):
            has[blk] = 0
            last[blk] = 0
            first = n

            def visit(s, n):
                hit = picked[s] == blk

                @pl.when(hit)
                def _():
                    order[n] = s
                    keep[n] = jnp.where(n == first, 0, 1)
                    last[blk] = n
                    has[blk] = 1

                return n + jnp.where(hit, 1, 0)

            return lax.fori_loop(0, GRP, visit, n)

        used = lax.fori_loop(0, HD, by_block, 0)

        def rest(i, _):
            order[i] = 1
            keep[i] = 0
            return 0

        lax.fori_loop(used, GRP, rest, 0)

    qb, dob = q[0], do[0]
    slots = [None] + [slot[b * 8 + n] for n in range(nb - 1)]

    def key(n):
        return ko[0] if n == 0 else kg[slots[n]]

    def val(n):
        return vo[0] if n == 0 else vg[slots[n]]

    top = None
    for n in range(nb):
        s = dot(key(n), qb, 1, 1)
        e[n] = s
        m = jnp.max(s, axis=0, keepdims=True)
        top = m if top is None else jnp.maximum(top, m)
    total = None
    shift = top * SCALE
    for n in range(nb):
        x = jnp.exp(e[n] * SCALE - shift)
        e[n] = x
        t = jnp.sum(x, axis=0, keepdims=True)
        total = t if total is None else total + t
    inv = 1.0 / total
    out_t = None
    for n in range(nb):
        h = (e[n] * inv).astype(BF16)
        ph[n] = h
        o = dot(val(n), h, 0, 0)
        out_t = o if out_t is None else out_t + o
    delta = jnp.sum(out_t * dob.astype(F32).T, axis=0, keepdims=True)
    att[0] = out_t.T.astype(BF16)
    dq_t = None
    for n in range(nb):
        dp = dot(val(n), dob, 1, 1)
        ds = (e[n] * inv * (dp - delta)).astype(BF16)
        x = dot(key(n), ds, 0, 0)
        dq_t = x if dq_t is None else dq_t + x
        gk = dot(ds, qb, 1, 0)
        gv = dot(ph[n], dob, 1, 0)
        if n == 0:
            dko[0] = gk * SCALE
            dvo[0] = gv
        else:
            acc_k[slots[n]] += gk
            acc_v[slots[n]] += gv
    dq[0] = (dq_t * SCALE).T.astype(BF16)

    @pl.when(b == HD - 1)
    def _():
        def put(s, _):
            bk[s] = (acc_k[s] * SCALE).astype(BF16)
            bv[s] = acc_v[s].astype(BF16)
            return 0

        lax.fori_loop(0, GRP, put, 0)


def attend(slot, picked, qh, doh, kh, vh, kgot, vgot):
    smem = pl.BlockSpec(memory_space=pltpu.SMEM)
    blk = pl.BlockSpec((1, ROWS, W), lambda b: (b, 0, 0))
    whole = pl.BlockSpec(memory_space=pltpu.VMEM)
    tile = jax.ShapeDtypeStruct((HD, ROWS, W), BF16)
    wide = jax.ShapeDtypeStruct((HD, ROWS, W), F32)
    slots = jax.ShapeDtypeStruct((GRP, ROWS, W), BF16)
    table = jax.ShapeDtypeStruct((GRP,), jnp.int32)
    short = jax.ShapeDtypeStruct((HD,), jnp.int32)
    return pl.pallas_call(
        attend_kernel,
        name="attend",
        grid=(HD,),
        out_shape=(tile, tile, wide, wide, slots, slots, table, table, short, short),
        in_specs=[smem, smem, blk, blk, blk, blk, whole, whole],
        out_specs=(blk, blk, blk, blk, whole, whole, smem, smem, smem, smem),
        scratch_shapes=[
            pltpu.VMEM((GRP, ROWS, W), F32),
            pltpu.VMEM((GRP, ROWS, W), F32),
            pltpu.VMEM((9, ROWS, ROWS), F32),
            pltpu.VMEM((9, ROWS, ROWS), BF16),
        ],
        compiler_params=pltpu.CompilerParams(dimension_semantics=("arbitrary",), vmem_limit_bytes=56 << 20),
    )(slot, picked, qh, doh, kh, vh, kgot, vgot)


def give_kernel(order, keep, last, has, att, dq, dko, dvo, bk, bv, out_o, out_q, out_k, out_v, rk, rv0, rv1, run, tk, tv0, tv1, own_k, own_v, zs, zr, xs, xr, ls):
    g, z = lax.axis_index("grp"), lax.axis_index("hd")
    own_loads = [pltpu.make_async_copy(dko, own_k, ls.at[6]), pltpu.make_async_copy(dvo, own_v, ls.at[7])]
    for c in own_loads:
        c.start()
    greet(g, z)
    mine = pl.ds(pl.multiple_of(z * W, W), W)
    src = {"k": bk, "v": bv}
    recv = [rk, rv0, rv1]
    tiles = [tk, tv0, tv1]
    own = {"k": own_k, "v": own_v}
    out = {"k": out_k, "v": out_v}
    jobs = [(att, 0, ROWS, out_o), (dq, 0, ROWS, out_q)]
    jobs += [(tiles[p], r0, n, out[a]) for p, (a, r0, n) in enumerate(OUT_PARTS)]

    def xy_copy(p, i):
        a, r0, n = OUT_PARTS[p]
        r = XY_ORDER[i]
        return pltpu.make_async_remote_copy(
            src_ref=src[a].at[r, pl.ds(r0, n)],
            dst_ref=recv[p].at[opposite(r)],
            send_sem=xs.at[p, i],
            recv_sem=xr.at[p, i],
            device_id={"grp": xy_group(g, r), "hd": z},
            device_id_type=MESH,
        )

    def z_copy(j, i, d):
        s, r0, n, dst = jobs[j]
        t = (z + d) % HD
        return pltpu.make_async_remote_copy(
            src_ref=s.at[t],
            dst_ref=dst.at[pl.ds(r0, n), mine],
            send_sem=zs.at[j, i],
            recv_sem=zr.at[j, i],
            device_id={"grp": g, "hd": t},
            device_id_type=MESH,
        )

    def own_copy(j):
        s, r0, n, dst = jobs[j]
        return pltpu.make_async_copy(s.at[z], dst.at[pl.ds(r0, n), mine], ls.at[j])

    def z_start(j):
        own_copy(j).start()
        for i, d in enumerate(Z_ORDER):
            z_copy(j, i, d).start()

    for i in range(len(XY_ORDER)):
        xy_copy(0, i).start()
    z_start(0)
    for p in range(1, len(OUT_PARTS)):
        for i in range(len(XY_ORDER)):
            xy_copy(p, i).start()
    z_start(1)
    for c in own_loads:
        c.wait()
    for p, (a, r0, n) in enumerate(OUT_PARTS):
        for i in range(len(XY_ORDER)):
            xy_copy(p, i).wait_recv()
        for r1 in range(0, n, 64):
            rows = pl.ds(r1, 64)

            def step(i, acc):
                acc = acc * keep[i].astype(F32) + recv[p][order[i], rows].astype(F32)
                run[i, rows] = acc
                return acc

            lax.fori_loop(0, GRP - 1, step, jnp.zeros((64, W), F32))
        for blk in range(HD):
            extra = run[last[blk], pl.ds(0, n)] * has[blk].astype(F32)
            tiles[p][blk] = (own[a][blk, pl.ds(r0, n)] + extra).astype(BF16)
        z_start(2 + p)
    for j in range(len(jobs)):
        own_copy(j).wait()
        for i, d in enumerate(Z_ORDER):
            z_copy(j, i, d).wait_send()
            z_copy(j, i, d).wait_recv()
    for p in range(len(OUT_PARTS)):
        for i in range(len(XY_ORDER)):
            xy_copy(p, i).wait_send()


def give(tables, att, dq, dko, dvo, bk, bv):
    hbm = pl.BlockSpec(memory_space=pl.ANY)
    flat = jax.ShapeDtypeStruct((ROWS, HD * W), BF16)
    nj, np_ = len(OUT_PARTS) + 2, len(OUT_PARTS)
    dma = pltpu.SemaphoreType.DMA
    return pl.pallas_call(
        give_kernel,
        name="give",
        out_shape=(flat,) * 4,
        in_specs=[pl.BlockSpec(memory_space=pltpu.SMEM)] * 4 + [hbm] * 6,
        out_specs=(hbm,) * 4,
        scratch_shapes=[pltpu.VMEM((GRP, n, W), BF16) for _, _, n in OUT_PARTS]
        + [pltpu.VMEM((GRP, ROWS, W), F32)]
        + [pltpu.VMEM((HD, n, W), BF16) for _, _, n in OUT_PARTS]
        + [pltpu.VMEM((HD, ROWS, W), F32)] * 2
        + [dma((nj, 7)), dma((nj, 7)), dma((np_, 31)), dma((np_, 31)), dma((nj + 3,))],
        compiler_params=pltpu.CompilerParams(collective_id=1, has_side_effects=True),
    )(*tables, att, dq, dko, dvo, bk, bv)


def on_device(queries, keys, values, grad_out, neighbours):
    g = lax.axis_index("grp")
    listed = neighbours.reshape(GRP, -1)
    picked = jnp.max(jnp.where(listed // HD == g, listed % HD, -1), axis=1)
    own = lax.dynamic_slice_in_dim(listed, g, 1, axis=0)[0] // HD
    dy = (own // 8 - g // 8) % 4
    dx = ((own // 2) % 4 - (g // 2) % 4) % 4
    dc = (own % 2 - g % 2) % 2
    slot = dy * 8 + dx * 2 + dc
    places = jnp.arange(GRP, dtype=jnp.int32)
    r_group = (((g // 8 + places // 8) % 4) * 4 + ((g // 2) % 4 + (places // 2) % 4) % 4) * 2 + (g % 2 + places % 2) % 2
    hit = jnp.where(listed[None] // HD == g, listed[None] % HD, -1)
    picked_r = jnp.max(jnp.where((r_group[:, None] == places[None, :])[:, :, None], hit, -1), axis=(1, 2))
    qh, kh, vh, doh, kgot, vgot = gather(jnp.maximum(picked, 0), queries, keys, values, grad_out)
    att, dq, dko, dvo, bk, bv, *tables = attend(slot, picked_r, qh, doh, kh, vh, kgot, vgot)
    return tuple(give(tables, att, dq, dko, dvo, bk, bv))


def solution(mesh):
    part = P(("grp", "hd"), None)
    return jax.shard_map(
        on_device, mesh=mesh, in_specs=(part,) * 4 + (P(),), out_specs=(part,) * 4, check_vma=False
    )
```

time: 511 us -> 190 us (0.37)
  Pallas kernels: 0 us -> 179 us
  local copies, waits for them, and re-layouts: 122 us -> 6.41 us
  waiting for transfers between devices: 97.8 us -> 0 us
  other arithmetic: 90.5 us -> 3.39 us
  blocking collectives: 71.7 us -> 0 us
  matrix products: 68.5 us -> 0 us
  starting transfers between devices: 53.5 us -> 0 us
    pallas_call x0 -> x3, Pallas kernels: none -> 179 us  [the longest x1 70.6 us: give(): pl.pallas_call(give_kernel, name='give', out_shape=(flat,) * 4, in_specs=...]
    all_to_all x10 -> x0, waiting for transfers between devices: 97.8 us -> none  [the longest x1 27.1 us: on_device(): lax.all_to_all(send_keys, 'grp', split_axis=0, concat_axis=0, tiled=True)]
    all_to_all x2 -> x0, blocking collectives: 71.7 us -> none  [the longest x1 35.9 us: on_device(): lax.all_to_all(send_values, 'grp', split_axis=0, concat_axis=0, tiled=True)]
    dot_general x48 -> x0, matrix products: 68.5 us -> none  [the longest x8 17.9 us: finish_block(): jnp.einsum('hqk,qhd->khd', grad_scores, query_blk, preferred_element_type...]
    all_to_all x10 -> x0, starting transfers between devices: 53.5 us -> none  [the longest x1 9 us: on_device(): lax.all_to_all(values, 'hd', split_axis=1, concat_axis=0, tiled=True)]
    scatter-add x4 -> x0, other arithmetic: 51.2 us -> none  [the longest x2 38.3 us: on_device(): empty_slots.at[slot_index]]
    dynamic_update_slice x32 -> x0, local copies, waits for them, and re-layouts: 33.8 us -> none  [on_device(): lax.map(visit_joint, (query_tiles, grad_tiles, own_key_tiles, own_value_t...]
    slice x2 -> x0, local copies, waits for them, and re-layouts: 15.5 us -> none  [the longest x1 7.73 us: on_device(): grad_key[:, 1:].reshape(-1, block_rows, local_width)]
  transfers between devices with their start and end apart: 10 -> 0, of which waited for: 7 -> 0; matrix products, arithmetic and copies ran while one was open for 26% -> 0% of each run, Pallas kernels for 0% -> 0%
where the time goes in v1:
time: 190 us; the launch traced here: 189 us
  Pallas kernels  179 us (94%)
  local copies, waits for them, and re-layouts  6.41 us (3%)
  other arithmetic  3.39 us (2%)
    pallas_call x1, Pallas kernels, give(): pl.pallas_call(give_kernel, name='give', out_shape=(flat,) * 4, in_specs=...  70.6 us
    pallas_call x1, Pallas kernels, gather(): pl.pallas_call(gather_kernel, name='gather', out_shape=(tile, tile, tile,...  69.9 us
    pallas_call x1, Pallas kernels, attend(): pl.pallas_call(attend_kernel, name='attend', grid=(HD,), out_shape=(tile,...  38.4 us
    unnamed x9, local copies, waits for them, and re-layouts  6.23 us

profile of v1, /device:TPU:1, one launch (start us, length us, event | category | flops | bytes accessed | tf_op | source)
XLA Modules:
  0.0 189.4 jit_solution(7909015472774756234)
XLA Ops:
  0.7 0.7 fusion.6
  1.4 0.1 iota_compare_fusion
  1.5 0.1 reduce_max.27
  1.6 0.1 reduce_max.28
  1.7 0.5 broadcast_maximum_fusion.picked
  2.2 0.8 copy.10
  3.0 0.1 reshape.202
  3.2 0.6 fusion.9.slot
  3.7 1.4 select_reduce_fusion.picked
  5.1 69.9 %gather.1 = (bf16[8,256,128]{2,1,0:T(8,128)(2,1)}, bf16[8,256,128]{2,1,0:T(8,128)(2,1)}, bf16[8,256,128]{2,1,0:T(8,128)(2,1)}, bf16[8,256,128]{2,1,0:T(8,128)(2,...) custom-call(s32[32]{0:T(128)} %broadcast_maximum_fusion.picked, bf16[256,1024]{1,0:T(8,128)(2,1)} %q.1, ...), custom_call_target="tpu_custom_call" | custom-call | tf_op jit(solution)/shard_map/gather/pallas_call | solution.py:125
  75.0 38.4 %attend.1 = (bf16[8,256,128]{2,1,0:T(8,128)(2,1)}, bf16[8,256,128]{2,1,0:T(8,128)(2,1)}, f32[8,256,128]{2,1,0:T(8,128)}, f32[8,256,128]{2,1,0:T(8,128)}, bf16[32...) custom-call(s32[64]{0:T(128)} %fusion.9.slot, ...), custom_call_target="tpu_custom_call" | custom-call | tf_op jit(solution)/shard_map/attend/pallas_call | solution.py:245
  113.4 70.6 %give.1 = (bf16[256,1024]{1,0:T(8,128)(2,1)}, bf16[256,1024]{1,0:T(8,128)(2,1)}, bf16[256,1024]{1,0:T(8,128)(2,1)}, bf16[256,1024]{1,0:T(8,128)(2,1)}) custom-call(s32[32]{0:T(128)} %get-tuple-element.26.order, s32[32]{0:T(128)} %get-tuple-element.27.keep, s32[8]{0:T(128)} %get-tuple-element.28.last, s32[8]{0:T(128)} %get-tuple-element.29.has, ...), custom_call_target="tpu_custom_call" | custom-call | tf_op jit(solution)/shard_map/give/pallas_call | solution.py:350
  184.0 0.0 copy-start.1
  184.0 0.0 copy-start
  184.0 2.0 %copy.15 = bf16[256,1024]{1,0:T(8,128)(2,1)} copy(bf16[256,1024]{1,0:T(8,128)(2,1)} %get-tuple-element.40) | data formatting | bytes 1048576
  185.9 1.9 copy.16
  187.8 0.0 copy-done.1
  187.8 0.8 copy.17
  188.6 0.0 copy-done
  188.6 0.8 copy.18
  (2 shorter events, 0.0 us)
Async XLA Ops:
  184.0 3.8 %copy-start.1 = (bf16[256,1024]{1,0:T(8,128)(2,1)S(1)}, bf16[256,1024]{1,0:T(8,128)(2,1)}, u32[]{:S(2)}) copy-start(bf16[256,1024]{1,0:T(8,128)(2,1)} %get-tuple-element.42) | copy-start | bytes 1572868
  184.0 4.6 %copy-start = (bf16[256,1024]{1,0:T(8,128)(2,1)S(1)}, bf16[256,1024]{1,0:T(8,128)(2,1)}, u32[]{:S(2)}) copy-start(bf16[256,1024]{1,0:T(8,128)(2,1)} %get-tuple-element.43) | copy-start | bytes 1572868

commit v2 on v0

v2 whole, which is shorter than its diff:
```python
import jax
import jax.numpy as jnp
from jax import lax
from jax.experimental import pallas as pl
from jax.experimental.pallas import tpu as pltpu
from jax.sharding import PartitionSpec as P

MESH = pl.DeviceIdType.MESH
HD = 8
GRP = 32
ROWS = 256
W = 128
F32 = jnp.float32
BF16 = jnp.bfloat16
SCALE = W ** (-0.5)

PLACES = [(0, 1), (1, 0), (0, 3), (3, 0), (0, 2), (2, 0), (1, 1), (3, 3), (1, 3), (3, 1), (2, 2), (1, 2), (2, 1), (3, 2), (2, 3), (0, 0)]
XY_ORDER = [dy * 8 + dx * 2 + dc for dc in (0, 1) for dy, dx in PLACES if dy + dx + dc > 0]
Z_ORDER = [1, 7, 2, 6, 3, 5, 4]


def opposite(r):
    return ((4 - r // 8) % 4) * 8 + ((4 - (r // 2) % 4) % 4) * 2 + r % 2


def xy_group(g, r):
    c, x, y = g % 2, (g // 2) % 4, g // 8
    return (((y + r // 8) % 4) * 4 + (x + (r // 2) % 4) % 4) * 2 + (c + r % 2) % 2


def greet(g, z):
    barrier = pltpu.get_barrier_semaphore()
    for r in XY_ORDER:
        pl.semaphore_signal(barrier, inc=1, device_id={"grp": xy_group(g, r), "hd": z}, device_id_type=MESH)
    for d in Z_ORDER:
        pl.semaphore_signal(barrier, inc=1, device_id={"grp": g, "hd": (z + d) % HD}, device_id_type=MESH)
    pl.semaphore_wait(barrier, len(XY_ORDER) + len(Z_ORDER))


HALF = ROWS // 2
NB = 8
PAIRS = HD * NB

PICKED, SLOT, LISTER, FILL, ORDER, KEEP, LAST, HAS, END = 0, 32, 96, 224, 256, 288, 320, 328, 336


def dot(a, b, ca, cb):
    return lax.dot_general(a, b, (((ca,), (cb,)), ((), ())), preferred_element_type=F32)


def kernel(tab, q, k, v, do, out_o, out_q, out_k, out_v, *scr):
    (k0, k1, vv, qh, doh, sk0, sk1, sv, gk0, gk1, gv, probs, pair, own_k, own_v, give_v, give_k, back_v, back_k0, back_k1, run, att, dq,
     tv, tk0, tk1, zs, zr, xs, xr, ls) = scr
    g, z = lax.axis_index("grp"), lax.axis_index("hd")
    mine = pl.ds(pl.multiple_of(z * W, W), W)
    nxy = len(XY_ORDER)
    inward = [(k, 0, HALF, k0), (k, HALF, HALF, k1), (v, 0, ROWS, vv), (q, 0, ROWS, qh), (do, 0, ROWS, doh)]
    outward = [(att, 0, ROWS, out_o), (dq, 0, ROWS, out_q), (tv, 0, ROWS, out_v), (tk0, 0, HALF, out_k), (tk1, HALF, HALF, out_k)]
    across = [(sk0, 0, HALF, gk0), (sk1, 0, HALF, gk1), (sv, 0, ROWS, gv)]
    across += [(give_v, 0, ROWS, back_v), (give_k, 0, HALF, back_k0), (give_k, HALF, HALF, back_k1)]
    nin = len(inward)

    def z_copy(j, i):
        d = Z_ORDER[i]
        t = (z + d) % HD
        if j < nin:
            s, r0, n, to = inward[j]
            src, dst = s.at[pl.ds(r0, n), pl.ds(pl.multiple_of(t * W, W), W)], to.at[z]
        else:
            s, r0, n, to = outward[j - nin]
            src, dst = s.at[t], to.at[pl.ds(r0, n), mine]
        return pltpu.make_async_remote_copy(
            src_ref=src, dst_ref=dst, send_sem=zs.at[j, i], recv_sem=zr.at[j, i],
            device_id={"grp": g, "hd": t}, device_id_type=MESH,
        )

    def own_copy(j):
        if j < nin:
            s, r0, n, to = inward[j]
            return pltpu.make_async_copy(s.at[pl.ds(r0, n), mine], to.at[z], ls.at[j])
        s, r0, n, to = outward[j - nin]
        return pltpu.make_async_copy(s.at[z], to.at[pl.ds(r0, n), mine], ls.at[j])

    def z_start(j):
        own_copy(j).start()
        for i in range(len(Z_ORDER)):
            z_copy(j, i).start()

    def z_arrive(j):
        own_copy(j).wait()
        for i in range(len(Z_ORDER)):
            z_copy(j, i).wait_recv()

    def xy_copy(p, i):
        s, r0, n, to = across[p]
        r = XY_ORDER[i]
        return pltpu.make_async_remote_copy(
            src_ref=s.at[r, pl.ds(r0, n)], dst_ref=to.at[opposite(r)],
            send_sem=xs.at[p, i], recv_sem=xr.at[p, i],
            device_id={"grp": xy_group(g, r), "hd": z}, device_id_type=MESH,
        )

    def xy_start(p):
        for i in range(nxy):
            xy_copy(p, i).start()

    def xy_arrive(p):
        for i in range(nxy):
            xy_copy(p, i).wait_recv()

    greet(g, z)
    for j in range(nin):
        z_start(j)
    for p, buf in enumerate((k0, k1, vv)):
        z_arrive(p)
        for r in XY_ORDER:
            across[p][0][r] = buf[tab[PICKED + xy_group(g, r)]]
        xy_start(p)
    z_arrive(3)
    z_arrive(4)
    xy_arrive(0)
    xy_arrive(1)

    def slots_of(b):
        return [None] + [tab[SLOT + b * NB + n] for n in range(NB)]

    def keys_of(b, slots, n):
        if n == 0:
            return jnp.concatenate([k0[b], k1[b]], axis=0)
        return jnp.concatenate([gk0[slots[n]], gk1[slots[n]]], axis=0)

    def values_of(b, slots, n):
        return vv[b] if n == 0 else gv[slots[n]]

    def first_half(b, _):
        slots = slots_of(b)
        qb, dob = qh[b], doh[b]
        top = None
        scores = []
        for n in range(NB + 1):
            s = dot(keys_of(b, slots, n), qb, 1, 1)
            run[n // 2, :, pl.ds((n % 2) * ROWS, ROWS)] = s
            m = jnp.max(s, axis=0, keepdims=True)
            top = m if top is None else jnp.maximum(top, m)
        shift = top * SCALE
        total = None
        for n in range(NB + 1):
            at = (n // 2, slice(None), pl.ds((n % 2) * ROWS, ROWS))
            x = jnp.exp(run[at] * SCALE - shift)
            run[at] = x
            t = jnp.sum(x, axis=0, keepdims=True)
            total = t if total is None else total + t
        inv = 1.0 / total
        for n in range(NB + 1):
            h = (run[n // 2, :, pl.ds((n % 2) * ROWS, ROWS)] * inv).astype(BF16)
            probs[b, n] = h
            x = dot(h, dob, 1, 0)
            if n == 0:
                own_v[b] = x
            else:
                pair[b * NB + n - 1] = x
        return 0

    lax.fori_loop(0, HD, first_half, 0)

    def collect(to, scale):
        def one(r, _):
            f = tab[FILL + r].astype(F32) * scale
            for r0 in range(0, ROWS, HALF):
                rows = pl.ds(r0, HALF)
                x = pair[tab[LISTER + r * 4], rows]
                for m in range(1, 4):
                    x = x + pair[tab[LISTER + r * 4 + m], rows]
                to[r, rows] = (x * f).astype(BF16)
            return 0

        lax.fori_loop(1, GRP, one, 0)

    collect(give_v, 1.0)
    xy_start(3)
    xy_arrive(2)

    def second_half(b, _):
        slots = slots_of(b)
        qb, dob = qh[b], doh[b]
        out_t = None
        for n in range(NB + 1):
            o = dot(values_of(b, slots, n), probs[b, n], 0, 0)
            out_t = o if out_t is None else out_t + o
        delta = jnp.sum(out_t * dob.astype(F32).T, axis=0, keepdims=True)
        att[b] = out_t.T.astype(BF16)
        dq_t = None
        for n in range(NB + 1):
            dp = dot(values_of(b, slots, n), dob, 1, 1)
            ds = (probs[b, n].astype(F32) * (dp - delta)).astype(BF16)
            x = dot(keys_of(b, slots, n), ds, 0, 0)
            dq_t = x if dq_t is None else dq_t + x
            x = dot(ds, qb, 1, 0)
            if n == 0:
                own_k[b] = x * SCALE
            else:
                pair[b * NB + n - 1] = x
        dq[b] = (dq_t * SCALE).T.astype(BF16)
        return 0

    lax.fori_loop(0, HD, second_half, 0)
    collect(give_k, SCALE)
    xy_start(4)
    xy_start(5)
    z_start(nin)
    z_start(nin + 1)
    totals = [(3, back_v, own_v, tv, 0, ROWS), (4, back_k0, own_k, tk0, 0, HALF), (5, back_k1, own_k, tk1, HALF, HALF)]
    for i, (p, back, own, tile, r0, n) in enumerate(totals):
        xy_arrive(p)
        for r1 in range(0, n, 64):
            rows = pl.ds(r1, 64)

            def step(m, acc):
                acc = acc * tab[KEEP + m].astype(F32) + back[tab[ORDER + m], rows].astype(F32)
                pair[m, rows] = acc
                return acc

            lax.fori_loop(0, GRP - 1, step, jnp.zeros((64, W), F32))
        for blk in range(HD):
            extra = pair[tab[LAST + blk], pl.ds(0, n)] * tab[HAS + blk].astype(F32)
            tile[blk] = (own[blk, pl.ds(r0, n)] + extra).astype(BF16)
        z_start(nin + 2 + i)
    for j in range(nin, nin + len(outward)):
        z_arrive(j)
    for j in range(nin + len(outward)):
        for i in range(len(Z_ORDER)):
            z_copy(j, i).wait_send()
    for p in range(len(across)):
        for i in range(nxy):
            xy_copy(p, i).wait_send()


def run_kernel(tab, q, k, v, do):
    hbm = pl.BlockSpec(memory_space=pl.ANY)
    flat = jax.ShapeDtypeStruct((ROWS, HD * W), BF16)
    dma = pltpu.SemaphoreType.DMA

    def tiles(n, rows=ROWS, dtype=BF16):
        return pltpu.VMEM((n, rows, W), dtype)

    return pl.pallas_call(
        kernel,
        name="graph_attention",
        out_shape=(flat,) * 4,
        in_specs=[pl.BlockSpec(memory_space=pltpu.SMEM)] + [hbm] * 4,
        out_specs=(hbm,) * 4,
        scratch_shapes=[
            tiles(HD, HALF), tiles(HD, HALF), tiles(HD), tiles(HD), tiles(HD),
            tiles(GRP, HALF), tiles(GRP, HALF), tiles(GRP), tiles(GRP, HALF), tiles(GRP, HALF), tiles(GRP),
            pltpu.VMEM((HD, NB + 1, ROWS, ROWS), BF16),
            tiles(PAIRS, ROWS, F32), tiles(HD, ROWS, F32), tiles(HD, ROWS, F32),
            tiles(GRP), tiles(GRP), tiles(GRP), tiles(GRP, HALF), tiles(GRP, HALF),
            pltpu.VMEM((5, ROWS, 2 * ROWS), F32),
            tiles(HD), tiles(HD), tiles(HD), tiles(HD, HALF), tiles(HD, HALF),
            dma((10, 7)), dma((10, 7)), dma((6, 31)), dma((6, 31)), dma((10,)),
        ],
        compiler_params=pltpu.CompilerParams(collective_id=0, has_side_effects=True, vmem_limit_bytes=62 << 20),
    )(tab, q, k, v, do)


def tables(neighbours):
    g = lax.axis_index("grp")
    listed = neighbours.reshape(GRP, -1)
    picked = jnp.max(jnp.where(listed // HD == g, listed % HD, -1), axis=1)
    places = jnp.arange(GRP, dtype=jnp.int32)
    r_group = xy_group(g, places)
    own = lax.dynamic_slice_in_dim(listed, g, 1, axis=0)[0] // HD
    slot = ((own // 8 - g // 8) % 4) * 8 + ((own // 2 - g // 2) % 4) * 2 + (own - g) % 2
    index = jnp.arange(PAIRS, dtype=jnp.int32)
    rank = jnp.sum((own[None, :] == own[:, None]) & (index[None, :] < index[:, None]), axis=1)
    mark = jnp.where(slot[None, :] == places[:, None], rank[None, :], -1)
    lister = jnp.max(jnp.where(mark[:, None, :] == jnp.arange(4)[None, :, None], index[None, None, :], 0), axis=2)
    fill = jnp.max(jnp.where(mark >= 0, 1, 0), axis=1)
    mine = jnp.max(jnp.where(r_group[:, None] == places[None, :], picked[None, :], -1), axis=1)
    block = jnp.where(places == 0, HD + 1, jnp.where(mine < 0, HD, mine))
    sort = block * GRP + places
    pos = jnp.sum(sort[None, :] < sort[:, None], axis=1)
    at = pos[None, :] == places[:, None]
    order = jnp.sum(jnp.where(at, places[None, :], 0), axis=1)
    sorted_block = jnp.sum(jnp.where(at, block[None, :], 0), axis=1)
    keep = jnp.sum(jnp.where((pos[None, :] + 1 == places[:, None]) & (block[None, :] == sorted_block[:, None]), 1, 0), axis=1)
    blocks = jnp.arange(HD, dtype=jnp.int32)
    upto = jnp.sum(block[None, :] <= blocks[:, None], axis=1)
    has = jnp.max(jnp.where(block[None, :] == blocks[:, None], 1, 0), axis=1)
    parts = [jnp.maximum(picked, 0), slot, lister.reshape(-1), fill, order, keep, jnp.maximum(upto - 1, 0), has]
    return jnp.concatenate([x.astype(jnp.int32) for x in parts])


def on_device(queries, keys, values, grad_out, neighbours):
    return tuple(run_kernel(tables(neighbours), queries, keys, values, grad_out))


def solution(mesh):
    part = P(("grp", "hd"), None)
    return jax.shard_map(
        on_device, mesh=mesh, in_specs=(part,) * 4 + (P(),), out_specs=(part,) * 4, check_vma=False
    )
```

time: 511 us -> 154 us (0.30)
  Pallas kernels: 0 us -> 144 us
  local copies, waits for them, and re-layouts: 122 us -> 7.02 us
  waiting for transfers between devices: 97.8 us -> 0 us
  other arithmetic: 90.5 us -> 1.53 us
  blocking collectives: 71.7 us -> 0 us
  matrix products: 68.5 us -> 0 us
  starting transfers between devices: 53.5 us -> 0 us
    pallas_call x0 -> x1, Pallas kernels: none -> 144 us  [run_kernel(): pl.pallas_call(kernel, name='graph_attention', out_shape=(flat,) * 4, in_...]
    all_to_all x10 -> x0, waiting for transfers between devices: 97.8 us -> none  [the longest x1 27.1 us: on_device(): lax.all_to_all(send_keys, 'grp', split_axis=0, concat_axis=0, tiled=True)]
    all_to_all x2 -> x0, blocking collectives: 71.7 us -> none  [the longest x1 35.9 us: on_device(): lax.all_to_all(send_values, 'grp', split_axis=0, concat_axis=0, tiled=True)]
    dot_general x48 -> x0, matrix products: 68.5 us -> none  [the longest x8 17.9 us: finish_block(): jnp.einsum('hqk,qhd->khd', grad_scores, query_blk, preferred_element_type...]
    all_to_all x10 -> x0, starting transfers between devices: 53.5 us -> none  [the longest x1 9 us: on_device(): lax.all_to_all(values, 'hd', split_axis=1, concat_axis=0, tiled=True)]
    scatter-add x4 -> x0, other arithmetic: 51.2 us -> none  [the longest x2 38.3 us: on_device(): empty_slots.at[slot_index]]
    dynamic_update_slice x32 -> x0, local copies, waits for them, and re-layouts: 33.8 us -> none  [on_device(): lax.map(visit_joint, (query_tiles, grad_tiles, own_key_tiles, own_value_t...]
    slice x2 -> x0, local copies, waits for them, and re-layouts: 15.5 us -> none  [the longest x1 7.73 us: on_device(): grad_key[:, 1:].reshape(-1, block_rows, local_width)]
  transfers between devices with their start and end apart: 10 -> 0, of which waited for: 7 -> 0; matrix products, arithmetic and copies ran while one was open for 26% -> 0% of each run, Pallas kernels for 0% -> 0%
where the time goes in v2:
time: 154 us; the launch traced here: 153 us
  Pallas kernels  144 us (94%)
  local copies, waits for them, and re-layouts  7.02 us (5%)
    pallas_call x1, Pallas kernels, run_kernel(): pl.pallas_call(kernel, name='graph_attention', out_shape=(flat,) * 4, in_...  144 us
    unnamed x13, local copies, waits for them, and re-layouts  5.97 us

profile of v2, /device:TPU:1, one launch (start us, length us, event | category | flops | bytes accessed | tf_op | source)
XLA Modules:
  0.0 153.4 jit_solution(2258322088672861562)
XLA Ops:
  0.7 0.0 copy-start.3
  0.7 0.7 copy-done.3
  1.4 0.1 reduce_max.53
  1.5 0.1 reduce_max.54
  1.6 0.2 select_reduce_fusion.4
  1.8 0.2 convert_reduce_fusion.1
  2.0 0.1 select_reduce_fusion.2
  2.1 0.2 select_reduce_fusion.1
  2.3 0.2 select_reduce_fusion.6
  2.5 0.1 copy.10
  2.6 0.1 reshape.187
  2.8 0.2 convert_reduce_fusion
  3.0 0.1 select_reduce_fusion.5
  3.1 0.1 select_reduce_fusion
  3.2 0.1 copy.11
  3.3 0.1 reshape.188
  3.4 0.7 concatenate.3.tab
  4.1 144.1 %graph_attention.1 = (bf16[256,1024]{1,0:T(8,128)(2,1)}, bf16[256,1024]{1,0:T(8,128)(2,1)}, bf16[256,1024]{1,0:T(8,128)(2,1)}, bf16[256,1024]{1,0:T(8,128)(2,1)}) custom-call(s32[336]{0:T(512)} %concatenate.3.tab, bf16[256,1024]{1,0:T(8,128)(2,1)} %q.1, bf16[256,1024]{1,0:T(8,128)(2,1)} %k.1, bf16[256,1024]{1,0:T(8,128)(2,1)} %v.1, bf16[256,1024]{1,0:T(8,128)(2,1)} %do.1), custom_call_target="tpu_custom_call" | custom-call | tf_op jit(solution)/shard_map/graph_attention/pallas_call | solution.py:246
  148.2 0.0 copy-start.2
  148.3 1.9 %copy.16 = bf16[256,1024]{1,0:T(8,128)(2,1)} copy(bf16[256,1024]{1,0:T(8,128)(2,1)} %get-tuple-element.20) | data formatting | bytes 1048576
  150.2 0.0 copy-done.2
  150.2 0.0 copy-start.1
  150.2 0.8 copy.17
  151.0 0.4 copy-done.1
  151.4 0.0 copy-start
  151.4 0.8 copy.18
  152.2 0.4 copy-done
  152.7 0.8 copy.19
  (8 shorter events, 0.1 us)
Async XLA Ops:
  0.7 0.7 copy-start.3
  148.2 1.9 %copy-start.2 = (bf16[256,1024]{1,0:T(8,128)(2,1)S(1)}, bf16[256,1024]{1,0:T(8,128)(2,1)}, u32[]{:S(2)}) copy-start(bf16[256,1024]{1,0:T(8,128)(2,1)} %get-tuple-element.21) | copy-start | bytes 1572868
  150.2 1.2 copy-start.1
  151.4 1.2 copy-start

commit v3 on v2

--- a/solution.py
+++ b/solution.py
@@ -17,6 +17,10 @@
 PLACES = [(0, 1), (1, 0), (0, 3), (3, 0), (0, 2), (2, 0), (1, 1), (3, 3), (1, 3), (3, 1), (2, 2), (1, 2), (2, 1), (3, 2), (2, 3), (0, 0)]
 XY_ORDER = [dy * 8 + dx * 2 + dc for dc in (0, 1) for dy, dx in PLACES if dy + dx + dc > 0]
 Z_ORDER = [1, 7, 2, 6, 3, 5, 4]
+
+
+def z_dist(i):
+    return jnp.where(i == 7, 0, jnp.where(i % 2 == 0, i // 2 + 1, 7 - i // 2))
 
 
 def opposite(r):
@@ -61,14 +65,13 @@
     nin = len(inward)
 
     def z_copy(j, i):
-        d = Z_ORDER[i]
-        t = (z + d) % HD
+        t = (z + (Z_ORDER[i] if isinstance(i, int) else z_dist(i))) % HD
         if j < nin:
             s, r0, n, to = inward[j]
             src, dst = s.at[pl.ds(r0, n), pl.ds(pl.multiple_of(t * W, W), W)], to.at[z]
         else:
             s, r0, n, to = outward[j - nin]
-            src, dst = s.at[t], to.at[pl.ds(r0, n), mine]
+            src, dst = s.at[t], to.at[z, pl.ds(r0, n)]
         return pltpu.make_async_remote_copy(
             src_ref=src, dst_ref=dst, send_sem=zs.at[j, i], recv_sem=zr.at[j, i],
             device_id={"grp": g, "hd": t}, device_id_type=MESH,
@@ -79,7 +82,7 @@
             s, r0, n, to = inward[j]
             return pltpu.make_async_copy(s.at[pl.ds(r0, n), mine], to.at[z], ls.at[j])
         s, r0, n, to = outward[j - nin]
-        return pltpu.make_async_copy(s.at[z], to.at[pl.ds(r0, n), mine], ls.at[j])
+        return pltpu.make_async_copy(s.at[z], to.at[z, pl.ds(r0, n)], ls.at[j])
 
     def z_start(j):
         own_copy(j).start()
@@ -117,7 +120,6 @@
             across[p][0][r] = buf[tab[PICKED + xy_group(g, r)]]
         xy_start(p)
     z_arrive(3)
-    z_arrive(4)
     xy_arrive(0)
     xy_arrive(1)
 
@@ -134,7 +136,7 @@
 
     def first_half(b, _):
         slots = slots_of(b)
-        qb, dob = qh[b], doh[b]
+        qb = qh[b]
         top = None
         scores = []
         for n in range(NB + 1):
@@ -152,16 +154,23 @@
             total = t if total is None else total + t
         inv = 1.0 / total
         for n in range(NB + 1):
-            h = (run[n // 2, :, pl.ds((n % 2) * ROWS, ROWS)] * inv).astype(BF16)
-            probs[b, n] = h
-            x = dot(h, dob, 1, 0)
+            probs[b, n] = (run[n // 2, :, pl.ds((n % 2) * ROWS, ROWS)] * inv).astype(BF16)
+        return 0
+
+    lax.fori_loop(0, HD, first_half, 0)
+    z_arrive(4)
+
+    def value_grads(b, _):
+        dob = doh[b]
+        for n in range(NB + 1):
+            x = dot(probs[b, n], dob, 1, 0)
             if n == 0:
                 own_v[b] = x
             else:
                 pair[b * NB + n - 1] = x
         return 0
 
-    lax.fori_loop(0, HD, first_half, 0)
+    lax.fori_loop(0, HD, value_grads, 0)
 
     def collect(to, scale):
         def one(r, _):
@@ -180,7 +189,17 @@
     xy_start(3)
     xy_arrive(2)
 
-    def second_half(b, _):
+    def z_send(j, i):
+        @pl.when(i < 7)
+        def _():
+            z_copy(j, i).start()
+
+        @pl.when(i == 7)
+        def _():
+            own_copy(j).start()
+
+    def second_half(i, _):
+        b = (z + z_dist(i)) % HD
         slots = slots_of(b)
         qb, dob = qh[b], doh[b]
         out_t = None
@@ -189,6 +208,7 @@
             out_t = o if out_t is None else out_t + o
         delta = jnp.sum(out_t * dob.astype(F32).T, axis=0, keepdims=True)
         att[b] = out_t.T.astype(BF16)
+        z_send(nin, i)
         dq_t = None
         for n in range(NB + 1):
             dp = dot(values_of(b, slots, n), dob, 1, 1)
@@ -201,14 +221,13 @@
             else:
                 pair[b * NB + n - 1] = x
         dq[b] = (dq_t * SCALE).T.astype(BF16)
+        z_send(nin + 1, i)
         return 0
 
     lax.fori_loop(0, HD, second_half, 0)
     collect(give_k, SCALE)
     xy_start(4)
     xy_start(5)
-    z_start(nin)
-    z_start(nin + 1)
     totals = [(3, back_v, own_v, tv, 0, ROWS), (4, back_k0, own_k, tk0, 0, HALF), (5, back_k1, own_k, tk1, HALF, HALF)]
     for i, (p, back, own, tile, r0, n) in enumerate(totals):
         xy_arrive(p)
@@ -237,7 +256,7 @@
 
 def run_kernel(tab, q, k, v, do):
     hbm = pl.BlockSpec(memory_space=pl.ANY)
-    flat = jax.ShapeDtypeStruct((ROWS, HD * W), BF16)
+    by_head = jax.ShapeDtypeStruct((HD, ROWS, W), BF16)
     dma = pltpu.SemaphoreType.DMA
 
     def tiles(n, rows=ROWS, dtype=BF16):
@@ -246,7 +265,7 @@
     return pl.pallas_call(
         kernel,
         name="graph_attention",
-        out_shape=(flat,) * 4,
+        out_shape=(by_head,) * 4,
         in_specs=[pl.BlockSpec(memory_space=pltpu.SMEM)] + [hbm] * 4,
         out_specs=(hbm,) * 4,
         scratch_shapes=[
@@ -261,6 +280,26 @@
         ],
         compiler_params=pltpu.CompilerParams(collective_id=0, has_side_effects=True, vmem_limit_bytes=62 << 20),
     )(tab, q, k, v, do)
+
+
+def lay_kernel(*refs):
+    for src, dst in zip(refs[:4], refs[4:]):
+        for h in range(HD):
+            dst[:, h * W : (h + 1) * W] = src[h]
+
+
+def lay(tiles):
+    steps = 4
+    rows = ROWS // steps
+    return pl.pallas_call(
+        lay_kernel,
+        name="lay",
+        grid=(steps,),
+        out_shape=(jax.ShapeDtypeStruct((ROWS, HD * W), BF16),) * 4,
+        in_specs=[pl.BlockSpec((HD, rows, W), lambda i: (0, i, 0))] * 4,
+        out_specs=(pl.BlockSpec((rows, HD * W), lambda i: (i, 0)),) * 4,
+        compiler_params=pltpu.CompilerParams(dimension_semantics=("arbitrary",), vmem_limit_bytes=62 << 20),
+    )(*tiles)
 
 
 def tables(neighbours):
@@ -292,7 +331,7 @@
 
 
 def on_device(queries, keys, values, grad_out, neighbours):
-    return tuple(run_kernel(tables(neighbours), queries, keys, values, grad_out))
+    return tuple(lay(run_kernel(tables(neighbours), queries, keys, values, grad_out)))
 
 
 def solution(mesh):

time: 154 us -> 137 us (0.89)
  Pallas kernels: 144 us -> 132 us
  local copies, waits for them, and re-layouts: 7.02 us -> 1.84 us
    pallas_call x1 -> x2, Pallas kernels: 144 us -> 132 us  [the longest x1 128 us: run_kernel(): pl.pallas_call(kernel, name='graph_attention', out_shape=(by_head,) * 4,...]
    unnamed x13 -> x3, local copies, waits for them, and re-layouts: 5.97 us -> 0.79 us
where the time goes in v3:
time: 137 us; the launch traced here: 136 us
  Pallas kernels  132 us (96%)
  local copies, waits for them, and re-layouts  1.84 us (1%)
  other arithmetic  1.53 us (1%)
    pallas_call x1, Pallas kernels, run_kernel(): pl.pallas_call(kernel, name='graph_attention', out_shape=(by_head,) * 4,...  128 us
    pallas_call x1, Pallas kernels, lay(): pl.pallas_call(lay_kernel, name='lay', grid=(steps,), out_shape=(jax.Shap...  3.96 us

profile of v3, /device:TPU:1, one launch (start us, length us, event | category | flops | bytes accessed | tf_op | source)
XLA Modules:
  0.0 136.5 jit_solution(1219187208748034535)
XLA Ops:
  0.7 0.0 copy-start
  0.7 0.7 copy-done
  1.4 0.1 reduce_max.53
  1.5 0.1 reduce_max.54
  1.6 0.2 select_reduce_fusion.4
  1.8 0.2 convert_reduce_fusion.1
  2.0 0.1 select_reduce_fusion.2
  2.1 0.2 select_reduce_fusion.1
  2.3 0.2 select_reduce_fusion.6
  2.5 0.1 copy.10
  2.6 0.1 reshape.187
  2.8 0.2 convert_reduce_fusion
  3.0 0.1 select_reduce_fusion.5
  3.1 0.1 select_reduce_fusion
  3.2 0.1 copy.11
  3.3 0.1 reshape.188
  3.4 0.7 concatenate.3.tab
  4.1 128.4 %graph_attention.1 = (bf16[8,256,128]{2,1,0:T(8,128)(2,1)}, bf16[8,256,128]{2,1,0:T(8,128)(2,1)}, bf16[8,256,128]{2,1,0:T(8,128)(2,1)}, bf16[8,256,128]{2,1,0:T(8,128)(2,1)}) custom-call(s32[336]{0:T(512)} %concatenate.3.tab, bf16[256,1024]{1,0:T(8,128)(2,1)} %q.1, bf16[256,1024]{1,0:T(8,128)(2,1)} %k.1, bf16[256,1024]{1,0:T(8,128)(2,1)} %v.1, ...), custom_call_target="tpu_custom_call" | custom-call | tf_op jit(solution)/shard_map/graph_attention/pallas_call | solution.py:265
  132.5 4.0 %lay.1 = (bf16[256,1024]{1,0:T(8,128)(2,1)}, bf16[256,1024]{1,0:T(8,128)(2,1)}, bf16[256,1024]{1,0:T(8,128)(2,1)}, bf16[256,1024]{1,0:T(8,128)(2,1)}) custom-call(bf16[8,256,128]{2,1,0:T(8,128)(2,1)} %get-tuple-element.8.refs_0_, bf16[8,256,128]{2,1,0:T(8,128)(2,1)} %get-tuple-element.9.refs_1_, bf16[8,256,128]{2,1,0:T(8,128)(2,1)} %get-tuple-element.10.refs_2_, ...), custom_call_target="tpu_custom_call" | custom-call | tf_op jit(solution)/shard_map/lay/pallas_call | solution.py:294
  (8 shorter events, 0.1 us)
Async XLA Ops:
  0.7 0.7 copy-start

commit v4 on v3

v4 whole, which is shorter than its diff:
```python
import jax
import jax.numpy as jnp
from jax import lax
from jax.experimental import pallas as pl
from jax.experimental.pallas import tpu as pltpu
from jax.sharding import PartitionSpec as P

MESH = pl.DeviceIdType.MESH
HD = 8
GRP = 32
ROWS = 256
W = 128
F32 = jnp.float32
BF16 = jnp.bfloat16
SCALE = W ** (-0.5)

PLACES = [(0, 1), (1, 0), (0, 3), (3, 0), (0, 2), (2, 0), (1, 1), (3, 3), (1, 3), (3, 1), (2, 2), (1, 2), (2, 1), (3, 2), (2, 3), (0, 0)]
XY_ORDER = [dy * 8 + dx * 2 + dc for dc in (0, 1) for dy, dx in PLACES if dy + dx + dc > 0]
Z_ORDER = [1, 7, 2, 6, 3, 5, 4]


def z_dist(i):
    return jnp.where(i == 7, 0, jnp.where(i % 2 == 0, i // 2 + 1, 7 - i // 2))


def opposite(r):
    return ((4 - r // 8) % 4) * 8 + ((4 - (r // 2) % 4) % 4) * 2 + r % 2


def xy_group(g, r):
    c, x, y = g % 2, (g // 2) % 4, g // 8
    return (((y + r // 8) % 4) * 4 + (x + (r // 2) % 4) % 4) * 2 + (c + r % 2) % 2


def greet(g, z):
    barrier = pltpu.get_barrier_semaphore()
    for r in XY_ORDER:
        pl.semaphore_signal(barrier, inc=1, device_id={"grp": xy_group(g, r), "hd": z}, device_id_type=MESH)
    for d in Z_ORDER:
        pl.semaphore_signal(barrier, inc=1, device_id={"grp": g, "hd": (z + d) % HD}, device_id_type=MESH)


def met():
    pl.semaphore_wait(pltpu.get_barrier_semaphore(), len(XY_ORDER) + len(Z_ORDER))


NB = 8
PAIRS = HD * NB

INWARD = [("k", 0, 48), ("k", 48, 80), ("k", 128, 128), ("v", 0, 128), ("q", 0, 256), ("v", 128, 128), ("do", 0, 256)]
LISTED = [i for i, part in enumerate(INWARD) if part[0] in "kv"]
RETURN = [("v", 0, 128), ("v", 128, 128), ("k", 0, 128), ("k", 128, 64), ("k", 192, 64)]
NIN, NLIST, NRET = len(INWARD), len(LISTED), len(RETURN)

PICKED, LISTER, FILL, ORDER, KEEP, LAST, HAS = 0, 1, 5, 6, 7, 8, 9
SLOT_ROW = 32


def dot(a, b, ca, cb):
    return lax.dot_general(a, b, (((ca,), (cb,)), ((), ())), preferred_element_type=F32)


def index_table(g, lists, table):
    def iota(shape, dim):
        return lax.broadcasted_iota(jnp.int32, shape, dim)

    def down(x):
        return jnp.sum(x, axis=0, keepdims=True)

    def along(x):
        return jnp.sum(x, axis=1, keepdims=True)

    def most(x):
        return jnp.max(x, axis=1, keepdims=True)

    def ones(cond):
        return jnp.where(cond, 1, 0)

    def as_row(col):
        n = col.shape[0]
        return down(jnp.where(iota((n, n), 0) == iota((n, n), 1), col, 0))

    def place_of(blk):
        other = blk // HD
        dy = (other // 8 - g // 8 + 4) % 4
        dx = ((other // 2) % 4 - (g // 2) % 4 + 4) % 4
        return dy * 8 + dx * 2 + (other % 2 - g % 2 + 2) % 2

    nb = lists[...]
    best = jnp.max(jnp.where(nb // HD == g, nb % HD, -1), axis=0, keepdims=True)
    place = iota((GRP, 1), 0)
    by = iota((GRP, GRP * HD), 1) // HD
    picked = most(jnp.where(by == iota((GRP, GRP * HD), 0), best, -1))
    mine = most(jnp.where(by == xy_group(g, place), best, -1))
    lane = iota((NB, GRP * HD), 1)
    own = jnp.concatenate([along(jnp.where(lane == g * HD + b, nb, 0)) for b in range(HD)], axis=0)
    slot_col, slot_row = place_of(own), place_of(as_row(own))
    s64, l64 = iota((PAIRS, PAIRS), 0), iota((PAIRS, PAIRS), 1)
    rank = down(ones((slot_col == slot_row) & (s64 < l64)))
    mark = jnp.where(slot_row == iota((GRP, PAIRS), 0), rank, -1)
    lister = [most(jnp.where(mark == m, iota((GRP, PAIRS), 1), 0)) for m in range(4)]
    fill = most(ones(mark >= 0))
    s32, l32 = iota((GRP, GRP), 0), iota((GRP, GRP), 1)
    block = jnp.where(place == 0, HD + 1, jnp.where(mine < 0, HD, mine))
    block_row = as_row(block)
    key = block * GRP + place
    pos = down(ones(key < as_row(key)))
    at = pos == s32
    order = along(jnp.where(at, l32, 0))
    sorted_block = along(jnp.where(at, block_row, 0))
    keep = along(ones((pos + 1 == s32) & (block_row == sorted_block)))
    last = along(ones(block_row <= s32)) - 1
    has = most(ones(block_row == s32))
    cols = [jnp.maximum(picked, 0)] + lister + [fill, order, keep, jnp.maximum(last, 0), has]
    out = jnp.zeros((GRP, W), jnp.int32)
    for c, col in enumerate(cols):
        out = jnp.where(iota((GRP, W), 1) == c, col, out)
    table[pl.ds(0, GRP)] = out
    slots = jnp.concatenate([slot_row, jnp.zeros((1, W - PAIRS), jnp.int32)], axis=1)
    table[pl.ds(SLOT_ROW, 8)] = jnp.broadcast_to(slots, (8, W))


def kernel(lists, q, k, v, do, out_o, out_q, out_k, out_v, *scr):
    scr = list(scr)

    def take(n):
        got, scr[:] = scr[:n], scr[n:]
        return got

    landed = take(NIN)
    sent, got = take(NLIST), take(NLIST)
    give_v, give_k = take(2)
    back = take(NRET)
    sums = take(NRET)
    probs, pair, own_k, own_v, work, att, dq, table, tab, zs, zr, xs, xr, ls, ts = scr
    g, z = lax.axis_index("grp"), lax.axis_index("hd")
    mine = pl.ds(pl.multiple_of(z * W, W), W)
    ins = {"q": q, "k": k, "v": v, "do": do}
    outs = {"k": out_k, "v": out_v}
    gives = {"k": give_k, "v": give_v}
    inward = [(ins[a], r0, n, landed[i]) for i, (a, r0, n) in enumerate(INWARD)]
    outward = [(att, 0, ROWS, out_o), (dq, 0, ROWS, out_q)]
    outward += [(sums[i], r0, n, outs[a]) for i, (a, r0, n) in enumerate(RETURN)]
    across = [(sent[i], 0, INWARD[j][2], got[i]) for i, j in enumerate(LISTED)]
    across += [(gives[a], r0, n, back[i]) for i, (a, r0, n) in enumerate(RETURN)]
    job = {a: i for i, (a, _, _) in enumerate(INWARD)}

    def z_copy(j, i):
        t = (z + (Z_ORDER[i] if isinstance(i, int) else z_dist(i))) % HD
        if j < NIN:
            s, r0, n, to = inward[j]
            src, dst = s.at[pl.ds(r0, n), pl.ds(pl.multiple_of(t * W, W), W)], to.at[z]
        else:
            s, r0, n, to = outward[j - NIN]
            src, dst = s.at[t], to.at[z, pl.ds(r0, n)]
        return pltpu.make_async_remote_copy(
            src_ref=src, dst_ref=dst, send_sem=zs.at[j], recv_sem=zr.at[j],
            device_id={"grp": g, "hd": t}, device_id_type=MESH,
        )

    def own_copy(j):
        if j < NIN:
            s, r0, n, to = inward[j]
            return pltpu.make_async_copy(s.at[pl.ds(r0, n), mine], to.at[z], ls.at[j])
        s, r0, n, to = outward[j - NIN]
        return pltpu.make_async_copy(s.at[z], to.at[z, pl.ds(r0, n)], ls.at[j])

    def wait_bytes(ref, sem):
        pltpu.make_async_copy(ref, ref, sem).wait()

    def z_bytes(j):
        if j < NIN:
            return landed[j].at[pl.ds(0, 7)]
        return outward[j - NIN][0].at[pl.ds(0, 7)]

    def z_start(j):
        own_copy(j).start()
        for i in range(len(Z_ORDER)):
            z_copy(j, i).start()

    def z_arrive(j):
        own_copy(j).wait()
        wait_bytes(z_bytes(j), zr.at[j])

    def xy_copy(p, i):
        s, r0, n, to = across[p]
        r = XY_ORDER[i]
        return pltpu.make_async_remote_copy(
            src_ref=s.at[r, pl.ds(r0, n)], dst_ref=to.at[opposite(r)],
            send_sem=xs.at[p], recv_sem=xr.at[p],
            device_id={"grp": xy_group(g, r), "hd": z}, device_id_type=MESH,
        )

    def xy_bytes(p):
        return across[p][3].at[pl.ds(1, GRP - 1)]

    def xy_start(p):
        for i in range(len(XY_ORDER)):
            xy_copy(p, i).start()

    def xy_arrive(p):
        wait_bytes(xy_bytes(p), xr.at[p])

    greet(g, z)
    index_table(g, lists, table)
    to_tab = pltpu.make_async_copy(table, tab, ts.at[0])
    to_tab.start()
    met()
    for j in range(NIN):
        z_start(j)
    to_tab.wait()
    for p, j in enumerate(LISTED):
        z_arrive(j)
        for r in XY_ORDER:
            sent[p][r] = landed[j][tab[xy_group(g, r), PICKED] & (HD - 1)]
        xy_start(p)
        if j + 1 < NIN and INWARD[j + 1][0] == "q":
            z_arrive(j + 1)
    k_parts = [p for p, j in enumerate(LISTED) if INWARD[j][0] == "k"]
    v_parts = [p for p, j in enumerate(LISTED) if INWARD[j][0] == "v"]
    for p in k_parts:
        xy_arrive(p)
    qh, doh = landed[job["q"]], landed[job["do"]]

    def slots_of(b):
        return [None] + [tab[SLOT_ROW, b * NB + n] & (GRP - 1) for n in range(NB)]

    def rows_of(parts, b, slots, n):
        if n == 0:
            return jnp.concatenate([landed[LISTED[p]][b] for p in parts], axis=0)
        return jnp.concatenate([got[p][slots[n]] for p in parts], axis=0)

    def first_half(b, _):
        slots = slots_of(b)
        qb = qh[b]
        top = None
        for n in range(NB + 1):
            s = dot(rows_of(k_parts, b, slots, n), qb, 1, 1)
            work[n] = s
            m = jnp.max(s, axis=0, keepdims=True)
            top = m if top is None else jnp.maximum(top, m)
        shift = top * SCALE
        total = None
        for n in range(NB + 1):
            x = jnp.exp(work[n] * SCALE - shift)
            work[n] = x
            t = jnp.sum(x, axis=0, keepdims=True)
            total = t if total is None else total + t
        inv = 1.0 / total
        for n in range(NB + 1):
            probs[b, n] = (work[n] * inv).astype(BF16)
        return 0

    lax.fori_loop(0, HD, first_half, 0)
    z_arrive(job["do"])

    def collect(p, scale):
        to, r0, n, _ = across[p]
        rows = pl.ds(r0, n)

        def one(r, _):
            f = tab[r, FILL].astype(F32) * scale
            x = pair[tab[r, LISTER] & (PAIRS - 1), rows]
            for m in range(1, 4):
                x = x + pair[tab[r, LISTER + m] & (PAIRS - 1), rows]
            to[r, rows] = (x * f).astype(BF16)
            return 0

        lax.fori_loop(1, GRP, one, 0)

    for i, (a, r0, nr) in enumerate(RETURN):
        if a == "v":
            rows = pl.ds(r0, nr)

            def value_grads(b, _):
                dob = doh[b]
                for n in range(NB + 1):
                    x = dot(probs[b, n, rows], dob, 1, 0)
                    if n == 0:
                        own_v[b, rows] = x
                    else:
                        pair[b * NB + n - 1, rows] = x
                return 0

            lax.fori_loop(0, HD, value_grads, 0)
            collect(NLIST + i, 1.0)
            xy_start(NLIST + i)
    for p in v_parts:
        xy_arrive(p)

    def z_send(j, i):
        @pl.when(i < 7)
        def _():
            z_copy(j, i).start()

        @pl.when(i == 7)
        def _():
            own_copy(j).start()

    def second_half(i, _):
        b = (z + z_dist(i)) % HD
        slots = slots_of(b)
        qb, dob = qh[b], doh[b]
        out_t = None
        for n in range(NB + 1):
            o = dot(rows_of(v_parts, b, slots, n), probs[b, n], 0, 0)
            out_t = o if out_t is None else out_t + o
        delta = jnp.sum(out_t * dob.astype(F32).T, axis=0, keepdims=True)
        att[b] = out_t.T.astype(BF16)
        z_send(NIN, i)
        dq_t = None
        for n in range(NB + 1):
            dp = dot(rows_of(v_parts, b, slots, n), dob, 1, 1)
            ds = (probs[b, n].astype(F32) * (dp - delta)).astype(BF16)
            x = dot(rows_of(k_parts, b, slots, n), ds, 0, 0)
            dq_t = x if dq_t is None else dq_t + x
            x = dot(ds, qb, 1, 0)
            if n == 0:
                own_k[b] = x * SCALE
            else:
                pair[b * NB + n - 1] = x
        dq[b] = (dq_t * SCALE).T.astype(BF16)
        z_send(NIN + 1, i)
        return 0

    lax.fori_loop(0, HD, second_half, 0)
    for i, (a, r0, n) in enumerate(RETURN):
        if a == "k":
            collect(NLIST + i, SCALE)
            xy_start(NLIST + i)
    owns = {"k": own_k, "v": own_v}
    for i, (a, r0, n) in enumerate(RETURN):
        xy_arrive(NLIST + i)
        for r1 in range(0, n, 64):
            rows = pl.ds(r1, 64)

            def step(m, acc):
                acc = acc * tab[m, KEEP].astype(F32) + back[i][tab[m, ORDER] & (GRP - 1), rows].astype(F32)
                pair[m, rows] = acc
                return acc

            lax.fori_loop(0, GRP - 1, step, jnp.zeros((64, W), F32))
        for blk in range(HD):
            extra = pair[tab[blk, LAST] & (GRP - 1), pl.ds(0, n)] * tab[blk, HAS].astype(F32)
            sums[i][blk] = (owns[a][blk, pl.ds(r0, n)] + extra).astype(BF16)
        z_start(NIN + 2 + i)
    for j in range(NIN, NIN + len(outward)):
        z_arrive(j)
    for j in range(NIN + len(outward)):
        wait_bytes(z_bytes(j), zs.at[j])
    for p in range(len(across)):
        wait_bytes(xy_bytes(p), xs.at[p])


def run_kernel(lists, q, k, v, do):
    hbm = pl.BlockSpec(memory_space=pl.ANY)
    by_head = jax.ShapeDtypeStruct((HD, ROWS, W), BF16)
    dma = pltpu.SemaphoreType.DMA

    def tiles(n, rows=ROWS, dtype=BF16):
        return pltpu.VMEM((n, rows, W), dtype)

    nz, nx = NIN + 2 + NRET, NLIST + NRET
    return pl.pallas_call(
        kernel,
        name="graph_attention",
        out_shape=(by_head,) * 4,
        in_specs=[pl.BlockSpec(memory_space=pltpu.VMEM)] + [hbm] * 4,
        out_specs=(hbm,) * 4,
        scratch_shapes=[tiles(HD, n) for _, _, n in INWARD]
        + [tiles(GRP, INWARD[j][2]) for j in LISTED] * 2
        + [tiles(GRP), tiles(GRP)]
        + [tiles(GRP, n) for _, _, n in RETURN]
        + [tiles(HD, n) for _, _, n in RETURN]
        + [
            pltpu.VMEM((HD, NB + 1, ROWS, ROWS), BF16),
            tiles(PAIRS, ROWS, F32), tiles(HD, ROWS, F32), tiles(HD, ROWS, F32),
            pltpu.VMEM((NB + 1, ROWS, ROWS), F32),
            tiles(HD), tiles(HD),
            pltpu.VMEM((40, W), jnp.int32),
            pltpu.SMEM((40, W), jnp.int32),
            dma((nz,)), dma((nz,)), dma((nx,)), dma((nx,)), dma((nz,)), dma((1,)),
        ],
        compiler_params=pltpu.CompilerParams(collective_id=0, has_side_effects=True, vmem_limit_bytes=62 << 20),
    )(lists, q, k, v, do)


def lay_kernel(*refs):
    for src, dst in zip(refs[:4], refs[4:]):
        for h in range(HD):
            dst[:, h * W : (h + 1) * W] = src[h]


def lay(tiles):
    steps = 4
    rows = ROWS // steps
    return pl.pallas_call(
        lay_kernel,
        name="lay",
        grid=(steps,),
        out_shape=(jax.ShapeDtypeStruct((ROWS, HD * W), BF16),) * 4,
        in_specs=[pl.BlockSpec((HD, rows, W), lambda i: (0, i, 0))] * 4,
        out_specs=(pl.BlockSpec((rows, HD * W), lambda i: (i, 0)),) * 4,
        compiler_params=pltpu.CompilerParams(dimension_semantics=("arbitrary",), vmem_limit_bytes=62 << 20),
    )(*tiles)


def on_device(queries, keys, values, grad_out, neighbours):
    return tuple(lay(run_kernel(neighbours.T, queries, keys, values, grad_out)))


def solution(mesh):
    part = P(("grp", "hd"), None)
    return jax.shard_map(
        on_device, mesh=mesh, in_specs=(part,) * 4 + (P(),), out_specs=(part,) * 4, check_vma=False
    )
```

time: 137 us -> 124 us (0.905)
  Pallas kernels: 132 us -> 123 us
  local copies, waits for them, and re-layouts: 1.84 us -> 0 us
  other arithmetic: 1.53 us -> 0 us
    pallas_call x1, Pallas kernels: 128 us -> 119 us  [run_kernel(): pl.pallas_call(kernel, name='graph_attention', out_shape=(by_head,) * 4,...]
where the time goes in v4:
time: 124 us; the launch traced here: 123 us
  Pallas kernels  123 us (99%)
    pallas_call x1, Pallas kernels, run_kernel(): pl.pallas_call(kernel, name='graph_attention', out_shape=(by_head,) * 4,...  119 us
    pallas_call x1, Pallas kernels, lay(): pl.pallas_call(lay_kernel, name='lay', grid=(steps,), out_shape=(jax.Shap...  3.96 us

profile of v4, /device:TPU:1, one launch (start us, length us, event | category | flops | bytes accessed | tf_op | source)
XLA Modules:
  0.0 123.2 jit_solution(12614357927224918827)
XLA Ops:
  0.6 118.6 %graph_attention.1 = (bf16[8,256,128]{2,1,0:T(8,128)(2,1)}, bf16[8,256,128]{2,1,0:T(8,128)(2,1)}, bf16[8,256,128]{2,1,0:T(8,128)(2,1)}, bf16[8,256,128]{2,1,0:T(8,128)(2,1)}) custom-call(s32[8,256]{1,0:T(8,128)} %bitcast.1, bf16[256,1024]{1,0:T(8,128)(2,1)} %q.1, bf16[256,1024]{1,0:T(8,128)(2,1)} %k.1, bf16[256,1024]{1,0:T(8,128)(2,1)} %v.1, ...), custom_call_target="tpu_custom_call" | custom-call | tf_op jit(solution)/shard_map/graph_attention/pallas_call | solution.py:364
  119.2 4.0 %lay.1 = (bf16[256,1024]{1,0:T(8,128)(2,1)}, bf16[256,1024]{1,0:T(8,128)(2,1)}, bf16[256,1024]{1,0:T(8,128)(2,1)}, bf16[256,1024]{1,0:T(8,128)(2,1)}) custom-call(bf16[8,256,128]{2,1,0:T(8,128)(2,1)} %get-tuple-element.8.refs_0_, bf16[8,256,128]{2,1,0:T(8,128)(2,1)} %get-tuple-element.9.refs_1_, bf16[8,256,128]{2,1,0:T(8,128)(2,1)} %get-tuple-element.10.refs_2_, ...), custom_call_target="tpu_custom_call" | custom-call | tf_op jit(solution)/shard_map/lay/pallas_call | solution.py:397

commit v5 on v4

--- a/solution.py
+++ b/solution.py
@@ -47,7 +47,7 @@
 NB = 8
 PAIRS = HD * NB
 
-INWARD = [("k", 0, 48), ("k", 48, 80), ("k", 128, 128), ("v", 0, 128), ("q", 0, 256), ("v", 128, 128), ("do", 0, 256)]
+INWARD = [("k", 0, 32), ("k", 32, 64), ("k", 96, 160), ("v", 0, 128), ("q", 0, 256), ("v", 128, 128), ("do", 0, 256)]
 LISTED = [i for i, part in enumerate(INWARD) if part[0] in "kv"]
 RETURN = [("v", 0, 128), ("v", 128, 128), ("k", 0, 128), ("k", 128, 64), ("k", 192, 64)]
 NIN, NLIST, NRET = len(INWARD), len(LISTED), len(RETURN)
@@ -132,7 +132,7 @@
     give_v, give_k = take(2)
     back = take(NRET)
     sums = take(NRET)
-    probs, pair, own_k, own_v, work, att, dq, table, tab, zs, zr, xs, xr, ls, ts = scr
+    probs, pair, own_k, own_v, work, deltas, att, dq, table, tab, zs, zr, xs, xr, ls, ts = scr
     g, z = lax.axis_index("grp"), lax.axis_index("hd")
     mine = pl.ds(pl.multiple_of(z * W, W), W)
     ins = {"q": q, "k": k, "v": v, "do": do}
@@ -206,7 +206,7 @@
     to_tab = pltpu.make_async_copy(table, tab, ts.at[0])
     to_tab.start()
     met()
-    for j in range(NIN):
+    for j in range(3):
         z_start(j)
     to_tab.wait()
     for p, j in enumerate(LISTED):
@@ -214,6 +214,9 @@
         for r in XY_ORDER:
             sent[p][r] = landed[j][tab[xy_group(g, r), PICKED] & (HD - 1)]
         xy_start(p)
+        if p == 0:
+            for later in range(3, NIN):
+                z_start(later)
         if j + 1 < NIN and INWARD[j + 1][0] == "q":
             z_arrive(j + 1)
     k_parts = [p for p, j in enumerate(LISTED) if INWARD[j][0] == "k"]
@@ -282,7 +285,7 @@
                         pair[b * NB + n - 1, rows] = x
                 return 0
 
-            lax.fori_loop(0, HD, value_grads, 0)
+            lax.fori_loop(0, HD, value_grads, 0, unroll=2)
             collect(NLIST + i, 1.0)
             xy_start(NLIST + i)
     for p in v_parts:
@@ -297,17 +300,26 @@
         def _():
             own_copy(j).start()
 
-    def second_half(i, _):
+    def outputs(i, _):
         b = (z + z_dist(i)) % HD
         slots = slots_of(b)
-        qb, dob = qh[b], doh[b]
+        dob = doh[b]
         out_t = None
         for n in range(NB + 1):
             o = dot(rows_of(v_parts, b, slots, n), probs[b, n], 0, 0)
             out_t = o if out_t is None else out_t + o
         delta = jnp.sum(out_t * dob.astype(F32).T, axis=0, keepdims=True)
         att[b] = out_t.T.astype(BF16)
+        deltas[b] = delta
         z_send(NIN, i)
+        return 0
+
+    lax.fori_loop(0, HD, outputs, 0, unroll=2)
+
+    def second_half(i, _):
+        b = (z + z_dist(i)) % HD
+        slots = slots_of(b)
+        qb, dob, delta = qh[b], doh[b], deltas[b]
         dq_t = None
         for n in range(NB + 1):
             dp = dot(rows_of(v_parts, b, slots, n), dob, 1, 1)
@@ -323,7 +335,7 @@
         z_send(NIN + 1, i)
         return 0
 
-    lax.fori_loop(0, HD, second_half, 0)
+    lax.fori_loop(0, HD, second_half, 0, unroll=2)
     for i, (a, r0, n) in enumerate(RETURN):
         if a == "k":
             collect(NLIST + i, SCALE)
@@ -376,6 +388,7 @@
             pltpu.VMEM((HD, NB + 1, ROWS, ROWS), BF16),
             tiles(PAIRS, ROWS, F32), tiles(HD, ROWS, F32), tiles(HD, ROWS, F32),
             pltpu.VMEM((NB + 1, ROWS, ROWS), F32),
+            pltpu.VMEM((HD, 1, ROWS), F32),
             tiles(HD), tiles(HD),
             pltpu.VMEM((40, W), jnp.int32),
             pltpu.SMEM((40, W), jnp.int32),
@@ -392,7 +405,7 @@
 
 
 def lay(tiles):
-    steps = 4
+    steps = 2
     rows = ROWS // steps
     return pl.pallas_call(
         lay_kernel,

time: 124 us -> 122 us (0.984)
  Pallas kernels: 123 us -> 121 us
where the time goes in v5:
time: 122 us
  Pallas kernels  121 us (99%)
    pallas_call x1, Pallas kernels, run_kernel(): pl.pallas_call(kernel, name='graph_attention', out_shape=(by_head,) * 4,...  119 us
    pallas_call x1, Pallas kernels, lay(): pl.pallas_call(lay_kernel, name='lay', grid=(steps,), out_shape=(jax.Shap...  2.8 us

profile of v5, /device:TPU:1, one launch (start us, length us, event | category | flops | bytes accessed | tf_op | source)
XLA Modules:
  0.0 122.0 jit_solution(11767547036246427337)
XLA Ops:
  0.6 118.6 %graph_attention.1 = (bf16[8,256,128]{2,1,0:T(8,128)(2,1)}, bf16[8,256,128]{2,1,0:T(8,128)(2,1)}, bf16[8,256,128]{2,1,0:T(8,128)(2,1)}, bf16[8,256,128]{2,1,0:T(8,128)(2,1)}) custom-call(s32[8,256]{1,0:T(8,128)} %bitcast.1, bf16[256,1024]{1,0:T(8,128)(2,1)} %q.1, bf16[256,1024]{1,0:T(8,128)(2,1)} %k.1, bf16[256,1024]{1,0:T(8,128)(2,1)} %v.1, ...), custom_call_target="tpu_custom_call" | custom-call | tf_op jit(solution)/shard_map/graph_attention/pallas_call | solution.py:376
  119.2 2.8 %lay.1 = (bf16[256,1024]{1,0:T(8,128)(2,1)}, bf16[256,1024]{1,0:T(8,128)(2,1)}, bf16[256,1024]{1,0:T(8,128)(2,1)}, bf16[256,1024]{1,0:T(8,128)(2,1)}) custom-call(bf16[8,256,128]{2,1,0:T(8,128)(2,1)} %get-tuple-element.8.refs_0_, bf16[8,256,128]{2,1,0:T(8,128)(2,1)} %get-tuple-element.9.refs_1_, bf16[8,256,128]{2,1,0:T(8,128)(2,1)} %get-tuple-element.10.refs_2_, ...), custom_call_target="tpu_custom_call" | custom-call | tf_op jit(solution)/shard_map/lay/pallas_call | solution.py:410

commit v6 on v5

--- a/solution.py
+++ b/solution.py
@@ -175,7 +175,7 @@
 
     def z_start(j):
         own_copy(j).start()
-        for i in range(len(Z_ORDER)):
+        for i in range(len(Z_ORDER))[::-1]:
             z_copy(j, i).start()
 
     def z_arrive(j):
@@ -195,7 +195,7 @@
         return across[p][3].at[pl.ds(1, GRP - 1)]
 
     def xy_start(p):
-        for i in range(len(XY_ORDER)):
+        for i in range(len(XY_ORDER))[::-1]:
             xy_copy(p, i).start()
 
     def xy_arrive(p):
@@ -269,7 +269,7 @@
             to[r, rows] = (x * f).astype(BF16)
             return 0
 
-        lax.fori_loop(1, GRP, one, 0)
+        lax.fori_loop(1, GRP, one, 0, unroll=4)
 
     for i, (a, r0, nr) in enumerate(RETURN):
         if a == "v":
@@ -351,7 +351,7 @@
                 pair[m, rows] = acc
                 return acc
 
-            lax.fori_loop(0, GRP - 1, step, jnp.zeros((64, W), F32))
+            lax.fori_loop(0, GRP - 1, step, jnp.zeros((64, W), F32), unroll=True)
         for blk in range(HD):
             extra = pair[tab[blk, LAST] & (GRP - 1), pl.ds(0, n)] * tab[blk, HAS].astype(F32)
             sums[i][blk] = (owns[a][blk, pl.ds(r0, n)] + extra).astype(BF16)

time: 122 us -> 118 us (0.967)
  Pallas kernels: 121 us -> 116 us
    pallas_call x1, Pallas kernels: 119 us -> 114 us  [run_kernel(): pl.pallas_call(kernel, name='graph_attention', out_shape=(by_head,) * 4,...]
where the time goes in v6:
time: 118 us; the launch traced here: 117 us
  Pallas kernels  116 us (98%)
    pallas_call x1, Pallas kernels, run_kernel(): pl.pallas_call(kernel, name='graph_attention', out_shape=(by_head,) * 4,...  114 us
    pallas_call x1, Pallas kernels, lay(): pl.pallas_call(lay_kernel, name='lay', grid=(steps,), out_shape=(jax.Shap...  2.8 us

profile of v6, /device:TPU:1, one launch (start us, length us, event | category | flops | bytes accessed | tf_op | source)
XLA Modules:
  0.0 117.0 jit_solution(16632466826998756905)
XLA Ops:
  0.6 113.5 %graph_attention.1 = (bf16[8,256,128]{2,1,0:T(8,128)(2,1)}, bf16[8,256,128]{2,1,0:T(8,128)(2,1)}, bf16[8,256,128]{2,1,0:T(8,128)(2,1)}, bf16[8,256,128]{2,1,0:T(8,128)(2,1)}) custom-call(s32[8,256]{1,0:T(8,128)} %bitcast.1, bf16[256,1024]{1,0:T(8,128)(2,1)} %q.1, bf16[256,1024]{1,0:T(8,128)(2,1)} %k.1, bf16[256,1024]{1,0:T(8,128)(2,1)} %v.1, ...), custom_call_target="tpu_custom_call" | custom-call | tf_op jit(solution)/shard_map/graph_attention/pallas_call | solution.py:376
  114.2 2.8 %lay.1 = (bf16[256,1024]{1,0:T(8,128)(2,1)}, bf16[256,1024]{1,0:T(8,128)(2,1)}, bf16[256,1024]{1,0:T(8,128)(2,1)}, bf16[256,1024]{1,0:T(8,128)(2,1)}) custom-call(bf16[8,256,128]{2,1,0:T(8,128)(2,1)} %get-tuple-element.8.refs_0_, bf16[8,256,128]{2,1,0:T(8,128)(2,1)} %get-tuple-element.9.refs_1_, bf16[8,256,128]{2,1,0:T(8,128)(2,1)} %get-tuple-element.10.refs_2_, ...), custom_call_target="tpu_custom_call" | custom-call | tf_op jit(solution)/shard_map/lay/pallas_call | solution.py:410
